TPU v7x, 32 devices: a whole 2x2x4 slice. The times are simulated.
32 devices in a mesh: groups: 2 (over y), space: 4 (over z), tm: 2 (over x), chan: 2 (over core).
Axes of the slice: x: 2, y: 2, z: 4, core: 2. Of those that a mesh axis runs over, the one named last changes fastest.
Arguments:
- hidden_states: bfloat16 [8, 4, 64, 512], P(('groups', 'tm'), 'space', None, 'chan'), parts along dimension 0, may hold values from -25 to 25
- first_gain: float32 [512], P('chan'), may hold values from 0.1 to 1.9
- second_gain: float32 [512], P('chan'), may hold values from 0.1 to 1.9
- query_weight: bfloat16 [512, 512], replicated, may hold values from -0.4861359 to 0.4861359
- key_weight: bfloat16 [512, 512], replicated, may hold values from -0.4861359 to 0.4861359
- value_weight: bfloat16 [512, 512], replicated, may hold values from -0.25 to 0.25
- out_weight: bfloat16 [512, 512], replicated, may hold values from -0.25 to 0.25
- conv_kernel: bfloat16 [3, 3, 3, 512, 512], P(None, None, None, 'tm', 'chan'), may hold values from -0.0546875 to 0.0546875
Outputs:
- attended: bfloat16 [8, 4, 64, 512], P(('groups', 'tm'), 'space', None, 'chan'), parts along dimension 0
- convolved: bfloat16 [8, 4, 64, 512], P(('groups', 'tm'), 'space', None, 'chan'), parts along dimension 0
There are 2 independent parts, one for each index of `groups`. A program takes and returns all parts, laid end to end along the dimension named above; an argument that names none is the same for every part. Nothing has to cross between parts.
All inputs are finite; a program needn't handle non-finite values.
Results may differ from a plain program's by a relative error of at most 0.012.
The roundings to bfloat16 on the way count: a program that leaves them out, or rounds other values in their place, can miss the bound.
Values may be sent and summed in bfloat16 or wider, within the bound.
A program may use at most 64 MiB of HBM per device.

v0:
```python
import functools

import jax
import jax.numpy as jnp
from jax import lax
from jax.experimental import pallas as pl
from jax.experimental.pallas import tpu as pltpu
from jax.sharding import PartitionSpec as P

D = 512
NGROUP = 32
EPSILON = 1e-06
LANES = 128
BLOCKS = D // LANES
GROUP = D // NGROUP
MESH = pl.DeviceIdType.MESH
REACH = 2
F32 = jnp.float32
BF16 = jnp.bfloat16


def group_total(v):
    lane = lax.broadcasted_iota(jnp.int32, v.shape, 1)
    width = v.shape[1]
    step = 1
    while step < GROUP:
        above = pltpu.roll(v, width - step, 1)
        below = pltpu.roll(v, step, 1)
        v = v + jnp.where((lane // step) % 2 == 0, above, below)
        step *= 2
    return v


def packed_moments(values, first_block):
    sums = jnp.sum(values, axis=0, keepdims=True)
    squares = jnp.sum(values * values, axis=0, keepdims=True)
    rows = jnp.concatenate([sums, squares] * 4, axis=0)
    totals = group_total(rows)
    place = lax.broadcasted_iota(jnp.int32, (1, LANES), 1) % GROUP
    packed = jnp.zeros((1, LANES), F32)
    for block in range(values.shape[1] // LANES):
        piece = totals[:, block * LANES : (block + 1) * LANES]
        packed = jnp.where(place == first_block + block, piece[0:1], packed)
        packed = jnp.where(place == BLOCKS + first_block + block, piece[1:2], packed)
    return packed


def moments(packed, population):
    place = lax.broadcasted_iota(jnp.int32, (2 * BLOCKS, LANES), 1) % GROUP
    row = lax.broadcasted_iota(jnp.int32, (2 * BLOCKS, LANES), 0)
    wide = jnp.broadcast_to(packed, (2 * BLOCKS, LANES))
    spread_out = group_total(jnp.where(place == row, wide, 0.0)) / population
    mean = jnp.concatenate([spread_out[k : k + 1] for k in range(BLOCKS)], axis=1)
    square = jnp.concatenate([spread_out[BLOCKS + k : BLOCKS + k + 1] for k in range(BLOCKS)], axis=1)
    variance = jnp.maximum(square - mean * mean, 0.0)
    return mean, lax.rsqrt(variance + EPSILON)


def kernel(
    S, T, C, W,
    x_hbm, g1, g2, wq_hbm, wk_hbm, wv_hbm, wo_hbm, wc_hbm,
    att_out, conv_out,
    x, wq, wk, wv, wo, wc,
    stat1_src, stat1, stat2_src, stat2, gall1, gall2,
    xall, tokens, keyed, valued, att_src, att_in, dsrc, dall, act, part_src, part,
    xload, wsem, send_sem, upsem, downsem, onsem, gsem, s1sem, xsem, s2sem, asem, dsem, psend, psem,
):
    g = lax.axis_index("groups")
    h = lax.axis_index("space")
    t = lax.axis_index("tm")
    c = lax.axis_index("chan")
    n = S * T * C
    me = (h * T + t) * C + c
    half = D // C
    Kc = D // T
    NF = T * C
    other = lax.rem(c + 1, C)

    def to_everyone(act_on):
        def tile(dh):
            row = lax.rem(h + dh, S)
            for dt in range(T):
                for dc in range(C):
                    act_on((g, row, lax.rem(t + dt, T), lax.rem(c + dc, C)))

        pl.loop(1, S, unroll=S <= 4)(tile)
        for dt in range(T):
            for dc in range(C):
                if dt or dc:
                    act_on((g, h, lax.rem(t + dt, T), lax.rem(c + dc, C)))

    first = [
        pltpu.make_async_copy(src, dst, xload.at[i])
        for i, (src, dst) in enumerate([(x_hbm, x), (g1, gall1.at[c]), (g2, gall2.at[c])])
    ]
    for load in first:
        load.start()
    barrier = pltpu.get_barrier_semaphore()

    to_everyone(
        lambda where: pl.semaphore_signal(barrier, inc=1, device_id=where, device_id_type=MESH)
    )

    loads = [
        pltpu.make_async_copy(src, dst, wsem.at[i])
        for i, (src, dst) in enumerate(
            [(wk_hbm, wk), (wq_hbm, wq), (wv_hbm, wv), (wo_hbm, wo), (wc_hbm, wc)]
        )
    ]
    for load in loads:
        load.start()

    for load in first:
        load.wait()
    own = x[...].reshape(C * W, half).astype(F32)
    stat1_src[...] = packed_moments(own, c * (half // LANES))
    stat1[me] = stat1_src[...]
    xall[h * C + c] = x[c, 0]
    pl.semaphore_wait(barrier, n - 1)

    def send_stat(src, dst, sends, recvs):
        to_everyone(
            lambda where: pltpu.make_async_remote_copy(
                src_ref=src, dst_ref=dst.at[me], send_sem=sends, recv_sem=recvs,
                device_id=where, device_id_type=MESH,
            ).start()
        )

    def drain(ref, sem):
        pltpu.make_async_copy(ref, ref, sem).wait()

    send_stat(stat1_src, stat1, send_sem.at[0], s1sem)
    gains = [
        pltpu.make_async_remote_copy(
            src_ref=src, dst_ref=dst.at[c], send_sem=send_sem.at[1 + k], recv_sem=gsem.at[k],
            device_id=(g, h, t, other), device_id_type=MESH,
        )
        for k, (src, dst) in enumerate([(g1, gall1), (g2, gall2)])
    ]
    for copy in gains:
        copy.start()
    def send_x(dh, dc, sem):
        frame = lax.rem(c + dc, C)
        pltpu.make_async_remote_copy(
            src_ref=x.at[frame, 0], dst_ref=xall.at[h * C + c], send_sem=sem, recv_sem=xsem.at[h],
            device_id=(g, h + dh, t, frame), device_id_type=MESH,
        ).start()

    reach = min(REACH, S - 1)
    for dc in range(1, C):
        send_x(0, dc, send_sem.at[3])
    for d in range(reach, 0, -1):

        @pl.when(h + d < S)
        def _():
            for dc in range(C):
                send_x(d, dc, upsem.at[d - 1])

        @pl.when(h >= d)
        def _():
            for dc in range(C):
                send_x(-d, dc, downsem.at[d - 1])

    def slots(r):
        return xall.at[pl.ds(r * C, C)]

    def hand_on(r, to, sem):
        return pltpu.make_async_remote_copy(
            src_ref=slots(r), dst_ref=slots(r), send_sem=sem, recv_sem=xsem.at[r],
            device_id=(g, to, t, c), device_id_type=MESH,
        )

    for d in range(reach, S - 1):

        @pl.when((h >= d) & (h < S - 1))
        def _():
            drain(slots(h - d), xsem.at[h - d])
            hand_on(h - d, h + 1, onsem.at[0, d]).start()

        @pl.when((h + d < S) & (h > 0))
        def _():
            drain(slots(h + d), xsem.at[h + d])
            hand_on(h + d, h - 1, onsem.at[1, d]).start()

    drain(stat1.at[pl.ds(0, n - 1)], s1sem)
    for copy in gains:
        copy.wait()
    population = float(n * W * GROUP)
    mean1, scale1 = moments(jnp.sum(stat1[...], axis=0), population)
    gain1 = jnp.concatenate([gall1[k] for k in range(C)], axis=1)
    gain2 = jnp.concatenate([gall2[k] for k in range(C)], axis=1)

    def row_tokens(r):
        pieces = []
        for k in range(C):
            lanes = slice(k * half, (k + 1) * half)
            value = xall[r * C + k].astype(F32)
            value = (value - mean1[:, lanes]) * scale1[:, lanes] * gain1[:, lanes]
            pieces.append(value.astype(BF16))
        return jnp.concatenate(pieces, axis=1)

    def project(first, stop):
        rows = tokens[first:stop].reshape((stop - first) * W, D)
        shape = (stop - first, W, D)
        keyed[first:stop] = jnp.dot(rows, wk[...], preferred_element_type=F32).astype(BF16).reshape(shape)
        valued[first:stop] = jnp.dot(rows, wv[...], preferred_element_type=F32).astype(BF16).reshape(shape)

    drain(xall.at[pl.ds(0, C - 1)], xsem.at[h])
    mine = row_tokens(h)
    loads[0].wait()
    loads[1].wait()
    loads[2].wait()
    queries = jnp.dot(mine, wq[...], preferred_element_type=F32).astype(BF16)
    tokens[0] = mine

    mirror = (2 * h) // S
    place_h = h + mirror * (S - 1 - 2 * h)
    for k in range(S - 1):
        r = k + (k - place_h + S) // S
        r = r + mirror * (S - 1 - 2 * r)

        @pl.when(jnp.logical_not(((r + reach <= h) & (h < S - 1)) | ((r >= h + reach) & (h > 0))))
        def _():
            drain(slots(r), xsem.at[r])

        tokens[k + 1] = row_tokens(r)

    project(0, S)

    scores = lax.dot_general(
        queries, keyed[...].reshape(S * W, D), (((1,), (1,)), ((), ())), preferred_element_type=F32
    ) * (D ** (-0.5))
    weights = jnp.exp(scores - jnp.max(scores, axis=1, keepdims=True))
    mass = jnp.sum(weights, axis=1, keepdims=True)
    mixed = jnp.dot(weights.astype(BF16), valued[...].reshape(S * W, D), preferred_element_type=F32)
    mixed = (mixed / mass).astype(BF16)
    loads[3].wait()
    attended = jnp.dot(mixed, wo[...], preferred_element_type=F32).astype(BF16)

    source = jnp.concatenate([xall[h * C + k] for k in range(C)], axis=1).astype(F32)
    resid = (source - mean1) + attended.astype(F32)
    for k in range(T):
        dsrc[k] = resid[:, k * Kc : (k + 1) * Kc].astype(BF16)
    for k in range(C):
        att_src[k] = attended[:, k * half : (k + 1) * half]
    stat2_src[...] = packed_moments(resid, 0)
    stat2[me] = stat2_src[...]
    send_stat(stat2_src, stat2, send_sem.at[4], s2sem)

    frame_at = t * C + c

    def send_rows(dh, skip_self):
        for dt in range(T):
            for dc in range(C):
                if skip_self and dt == 0 and dc == 0:
                    continue
                to = lax.rem(t + dt, T)
                pltpu.make_async_remote_copy(
                    src_ref=dsrc.at[to], dst_ref=dall.at[1 - dh, frame_at],
                    send_sem=send_sem.at[6 + dh], recv_sem=dsem.at[1 - dh],
                    device_id=(g, h + dh, to, lax.rem(c + dc, C)), device_id_type=MESH,
                ).start()

    @pl.when(h > 0)
    def _():
        send_rows(-1, False)

    @pl.when(h < S - 1)
    def _():
        send_rows(1, False)

    send_rows(0, True)
    back = pltpu.make_async_remote_copy(
        src_ref=att_src.at[other], dst_ref=att_in, send_sem=send_sem.at[8], recv_sem=asem,
        device_id=(g, h, t, other), device_id_type=MESH,
    )
    back.start()
    dall[1, frame_at] = dsrc[t]
    att_out[c, 0] = att_src[c]
    act[0:2] = jnp.zeros((2,) + act.shape[1:], BF16)

    drain(stat2.at[pl.ds(0, n - 1)], s2sem)
    mean2, scale2 = moments(jnp.sum(stat2[...], axis=0), population)
    factor = scale2 * gain2

    def sliced(v):
        out = v[:, 0:Kc]
        for k in range(1, T):
            out = jnp.where(t == k, v[:, k * Kc : (k + 1) * Kc], out)
        return out

    mean_t = sliced(mean2)
    factor_t = sliced(factor)
    column = lax.broadcasted_iota(jnp.int32, (W, Kc), 0)

    def activate(row):
        @pl.loop(0, NF, unroll=NF <= 4)
        def _(f):
            v = (dall[row, f].astype(F32) - mean_t) * factor_t
            a = v / (1.0 + jnp.exp(-v))
            left = jnp.where(column == 0, 0.0, pltpu.roll(a, 1, 0))
            right = jnp.where(column == W - 1, 0.0, pltpu.roll(a, W - 1, 0))
            for e, piece in enumerate((left, a, right)):
                k = row * 3 + e
                act[f + 2, :, k * Kc : (k + 1) * Kc] = piece.astype(BF16)

    def blank(row):
        act[2:, :, row * 3 * Kc : (row + 1) * 3 * Kc] = jnp.zeros((NF, W, 3 * Kc), BF16)

    drain(dall.at[1, pl.ds(0, NF - 1)], dsem.at[1])
    activate(1)

    @pl.when(h > 0)
    def _():
        drain(dall.at[0], dsem.at[0])
        activate(0)

    @pl.when(h == 0)
    def _():
        blank(0)

    @pl.when(h < S - 1)
    def _():
        drain(dall.at[2], dsem.at[2])
        activate(2)

    @pl.when(h == S - 1)
    def _():
        blank(2)

    loads[4].wait()

    def partial(to):
        total = None
        for a in range(3):
            window = act[pl.ds(to * C + a, C)].reshape(C * W, 9 * Kc)
            product = jnp.dot(window, wc[a], preferred_element_type=F32)
            total = product if total is None else total + product
        return total

    returns = []
    for dt in range(1, T):
        to = lax.rem(t + dt, T)
        part_src[dt - 1] = partial(to).astype(BF16)
        copy = pltpu.make_async_remote_copy(
            src_ref=part_src.at[dt - 1], dst_ref=part.at[dt - 1],
            send_sem=psend.at[dt - 1], recv_sem=psem.at[dt - 1],
            device_id=(g, h, to, c), device_id_type=MESH,
        )
        copy.start()
        returns.append(copy)
    total = partial(t)
    back.wait()
    att_out[other, 0] = att_in[...]

    drain(stat1.at[pl.ds(0, n - 1)], send_sem.at[0])
    drain(xall.at[pl.ds(0, C - 1)], send_sem.at[3])
    for d in range(1, reach + 1):

        @pl.when(h + d < S)
        def _():
            drain(slots(0), upsem.at[d - 1])

        @pl.when(h >= d)
        def _():
            drain(slots(0), downsem.at[d - 1])

    for d in range(reach, S - 1):

        @pl.when((h >= d) & (h < S - 1))
        def _():
            drain(slots(0), onsem.at[0, d])

        @pl.when((h + d < S) & (h > 0))
        def _():
            drain(slots(0), onsem.at[1, d])

    drain(stat2.at[pl.ds(0, n - 1)], send_sem.at[4])
    drain(dall.at[1, pl.ds(0, NF - 1)], send_sem.at[6])

    @pl.when(h > 0)
    def _():
        drain(dall.at[0], send_sem.at[5])

    @pl.when(h < S - 1)
    def _():
        drain(dall.at[2], send_sem.at[7])

    for k, copy in enumerate(returns):
        copy.wait()
        total = total + part[k].astype(F32)
    conv_out[...] = total.reshape(conv_out.shape).astype(BF16)


def hand_over(att_in, conv_in, att_out, conv_out):
    att_out[...] = att_in[...]
    conv_out[...] = conv_in[...]


def on_device(S, T, C, x, g1, g2, wq, wk, wv, wo, wc):
    frames, rows, W, half = x.shape
    assert frames == C and rows == 1 and half * C == D
    Kc = wc.shape[3]
    assert Kc * T == D
    n, NF = S * T * C, T * C
    wc = wc.reshape(3, 9 * Kc, half)
    vmem = pl.BlockSpec(memory_space=pltpu.VMEM)
    hbm = pl.BlockSpec(memory_space=pl.ANY)
    out = jax.ShapeDtypeStruct(x.shape, BF16)
    dma = pltpu.SemaphoreType.DMA
    kept = pltpu.VMEM(x.shape, BF16)
    results = pl.pallas_call(
        functools.partial(kernel, S, T, C, W),
        out_shape=(kept, kept),
        in_specs=[hbm] * 8,
        out_specs=(vmem, vmem),
        scratch_shapes=[
            pltpu.VMEM(x.shape, BF16),
            *[pltpu.VMEM((D, D), BF16)] * 4,
            pltpu.VMEM(wc.shape, BF16),
            pltpu.VMEM((1, LANES), F32),
            pltpu.VMEM((n, 1, LANES), F32),
            pltpu.VMEM((1, LANES), F32),
            pltpu.VMEM((n, 1, LANES), F32),
            pltpu.VMEM((C, 1, half), F32),
            pltpu.VMEM((C, 1, half), F32),
            pltpu.VMEM((S * C, W, half), BF16),
            *[pltpu.VMEM((S, W, D), BF16)] * 3,
            pltpu.VMEM((C, W, half), BF16),
            pltpu.VMEM((W, half), BF16),
            pltpu.VMEM((T, W, Kc), BF16),
            pltpu.VMEM((3, NF, W, Kc), BF16),
            pltpu.VMEM((NF + 2, W, 9 * Kc), BF16),
            pltpu.VMEM((max(T - 1, 1), C * W, half), BF16),
            pltpu.VMEM((max(T - 1, 1), C * W, half), BF16),
            dma((3,)),
            dma((5,)),
            dma((9,)),
            dma((REACH,)),
            dma((REACH,)),
            dma((2, S)),
            dma((2,)),
            dma(()),
            dma((S,)),
            dma(()),
            dma(()),
            dma((3,)),
            dma((max(T - 1, 1),)),
            dma((max(T - 1, 1),)),
        ],
        compiler_params=pltpu.CompilerParams(collective_id=0, has_side_effects=True),
    )(x, g1.reshape(1, half), g2.reshape(1, half), wq, wk, wv, wo, wc)
    return pl.pallas_call(
        hand_over, out_shape=(out, out), in_specs=[vmem] * 2, out_specs=(vmem, vmem),
    )(*[pltpu.with_memory_space_constraint(r, pltpu.VMEM) for r in results])


def solution(mesh):
    S, T, C = mesh.shape["space"], mesh.shape["tm"], mesh.shape["chan"]
    placed = (
        P(("groups", "tm"), "space", None, "chan"),
        P("chan"),
        P("chan"),
        P(),
        P(),
        P(),
        P(),
        P(None, None, None, "tm", "chan"),
    )
    return jax.shard_map(
        functools.partial(on_device, S, T, C),
        mesh=mesh,
        in_specs=placed,
        out_specs=(
            P(("groups", "tm"), "space", None, "chan"),
            P(("groups", "tm"), "space", None, "chan"),
        ),
        check_vma=False,
    )
```

profile of v0, /device:TPU:0, one launch (start us, length us, event | category | flops | bytes accessed | tf_op | source)
XLA Modules:
  0.0 25.6 jit_solution(13912787472694371595)
XLA Ops:
  0.6 24.3 %shard_map.95 = (bf16[2,1,64,256]{3,2,1,0:T(8,128)(2,1)S(1)}, bf16[2,1,64,256]{3,2,1,0:T(8,128)(2,1)S(1)}) custom-call(bf16[2,1,64,256]{3,2,1,0:T(8,128)(2,1)} %x_hbm.1, f32[1,256]{1,0:T(1,128)} %bitcast.4, f32[1,256]{1,0:T(1,128)} %bitcast.5, bf16[512,512]{1,0:T(8,128)(2,1)} %wq_hbm.1, bf16[512,512]{1,0:T(8,128)(2,1)} %wk_hbm.1, bf16[512,512]{1,0:T(8,128)(2,1)} %wv_hbm.1, ...), custom_call_target="tpu_custom_call" | custom-call | tf_op jit(solution)/shard_map/pallas_call | solution.py:412
  24.9 0.7 %shard_map.96 = (bf16[2,1,64,256]{3,2,1,0:T(8,128)(2,1)}, bf16[2,1,64,256]{3,2,1,0:T(8,128)(2,1)}) custom-call(bf16[2,1,64,256]{3,2,1,0:T(8,128)(2,1)S(1)} %get-tuple-element.4.att_in, bf16[2,1,64,256]{3,2,1,0:T(8,128)(2,1)S(1)} %get-tuple-element.5.conv_in), custom_call_target="tpu_custom_call" | custom-call | tf_op jit(solution)/shard_map/pallas_call | solution.py:453
where the time goes:
time: 25.7 us; the launch traced here: 25.6 us
  Pallas kernels  24.9 us (97%)
  between operations  0.64 us (2%)
    pallas_call x1, Pallas kernels, on_device(): pl.pallas_call(functools.partial(kernel, S, T, C, W), out_shape=(kept, ke...  24.3 us
    pallas_call x1, Pallas kernels, on_device(): pl.pallas_call(hand_over, out_shape=(out, out), in_specs=[vmem] * 2, out_...  0.66 us

commit v1 on v0

v1 whole, which is shorter than its diff:
```python
import functools

import jax
import jax.numpy as jnp
from jax import lax
from jax.experimental import pallas as pl
from jax.experimental.pallas import tpu as pltpu
from jax.sharding import PartitionSpec as P

D = 512
NGROUP = 32
EPSILON = 1e-06
LANES = 128
CHUNKS = 2
GROUP = D // NGROUP
MESH = pl.DeviceIdType.MESH
F32 = jnp.float32
BF16 = jnp.bfloat16


def group_total(v):
    lane = lax.broadcasted_iota(jnp.int32, v.shape, 1)
    width = v.shape[1]
    step = 1
    while step < GROUP:
        above = pltpu.roll(v, width - step, 1)
        below = pltpu.roll(v, step, 1)
        v = v + jnp.where((lane // step) % 2 == 0, above, below)
        step *= 2
    return v


def channel_sums(values):
    return jnp.sum(values, axis=0, keepdims=True), jnp.sum(values * values, axis=0, keepdims=True)


def moments(totals, population):
    blocks = totals.shape[1] // LANES
    pieces = [totals[k : k + 1, b * LANES : (b + 1) * LANES] for k in range(2) for b in range(blocks)]
    rows = 8 * pl.cdiv(2 * blocks, 8)
    grouped = group_total(jnp.concatenate(pieces + pieces[:1] * (rows - 2 * blocks), axis=0)) / population
    mean = jnp.concatenate([grouped[b : b + 1] for b in range(blocks)], axis=1)
    square = jnp.concatenate([grouped[blocks + b : blocks + b + 1] for b in range(blocks)], axis=1)
    variance = jnp.maximum(square - mean * mean, 0.0)
    return mean, lax.rsqrt(variance + EPSILON)


def kernel(
    S, T, C, W,
    x_hbm, g1, g2, wq_hbm, wk_hbm, wv_hbm, wo_hbm, wc_hbm,
    att_out, conv_out,
    x, wq, wk, wv, wo, wc,
    stat1_src, stat1, stat2_src, stat2, gall1, gall2,
    xall, tokens, keyed, valued, att_src, att_in, dsrc, dall, act, own_total, part_src, part,
    xload, wsem, insem, send_sem, gsem, s1send, s1sem, xsend, xsem, s2sem,
    asend, asem, dsend, dsem, last_sem, share_sem, psend, psem,
):
    g = lax.axis_index("groups")
    h = lax.axis_index("space")
    t = lax.axis_index("tm")
    c = lax.axis_index("chan")
    n = S * T * C
    chip = h * T + t
    me = chip * C + c
    half = D // C
    Kc = D // T
    NF = T * C
    other = lax.rem(c + 1, C)
    inner = (h > 0) & (h < S - 1)
    attends = h < S - 1

    def rows_apart(sign, act_on):
        def row(d):
            @pl.when((h + sign * d >= 0) & (h + sign * d < S))
            def _():
                act_on(h + sign * d, d)

        pl.loop(1, S, unroll=S <= 4)(row)

    def row_devices(r, act_on):
        for dt in range(T):
            for dc in range(C):
                act_on((g, r, lax.rem(t + dt, T), lax.rem(c + dc, C)))

    def beside(sign, act_on):
        for dt in range(1, T):

            @pl.when((t + sign * dt >= 0) & (t + sign * dt < T))
            def _():
                for dc in range(C):
                    act_on((g, h, t + sign * dt, lax.rem(c + dc, C)))

    def mates(act_on):
        for dc in range(1, C):
            act_on((g, h, t, lax.rem(c + dc, C)))

    def signal(sem):
        return lambda where: pl.semaphore_signal(sem, inc=1, device_id=where, device_id_type=MESH)

    def drain(ref, sem):
        pltpu.make_async_copy(ref, ref, sem).wait()

    first = [
        pltpu.make_async_copy(src, dst, xload.at[i])
        for i, (src, dst) in enumerate([(x_hbm, x), (g1, gall1.at[c]), (g2, gall2.at[c])])
    ]
    for load in first:
        load.start()
    barrier = pltpu.get_barrier_semaphore()
    mates(signal(barrier))
    beside(1, signal(barrier))
    rows_apart(1, lambda r, d: row_devices(r, signal(barrier)))
    pl.semaphore_wait(barrier, chip * C + C - 1)

    def answer(r, d):
        for dt in range(T):
            for dc in range(C):
                signal(insem.at[min(dt, 1), d])((g, r, lax.rem(t + dt, T), lax.rem(c + dc, C)))

    rows_apart(-1, answer)
    beside(-1, signal(insem.at[0, 0]))

    loads = [
        pltpu.make_async_copy(src, dst, wsem.at[i])
        for i, (src, dst) in enumerate(
            [(wk_hbm, wk), (wq_hbm, wq), (wv_hbm, wv), (wo_hbm, wo), (wc_hbm, wc)]
        )
    ]
    pl.when(attends)(lambda: [load.start() for load in loads[:4]] and None)
    loads[4].start()

    for load in first:
        load.wait()
    sums, squares = channel_sums(x[...].reshape(C * W, half).astype(F32))
    stat1_src[0:1] = sums
    stat1_src[1:2] = squares
    stat1[me] = stat1_src[...]
    xall[h * C + c] = x[c, 0]

    def send_stat(where):
        pltpu.make_async_remote_copy(
            src_ref=stat1_src, dst_ref=stat1.at[me], send_sem=s1send.at[where[1]], recv_sem=s1sem,
            device_id=where, device_id_type=MESH,
        ).start()

    def send_x(r, dc):
        frame = lax.rem(c + dc, C)
        pltpu.make_async_remote_copy(
            src_ref=x.at[frame, 0], dst_ref=xall.at[h * C + c], send_sem=xsend.at[r], recv_sem=xsem.at[h * C + c],
            device_id=(g, r, t, frame), device_id_type=MESH,
        ).start()

    def column_x(r):
        for dc in range(C):
            send_x(r, dc)

    rows_apart(-1, lambda r, d: row_devices(r, send_stat))

    @pl.when(attends)
    def _():
        beside(-1, send_stat)
        mates(send_stat)
        for dc in range(1, C):
            send_x(h, dc)

    rows_apart(-1, lambda r, d: column_x(r))

    gains = [
        pltpu.make_async_remote_copy(
            src_ref=src, dst_ref=dst.at[c], send_sem=send_sem.at[1 + k], recv_sem=gsem.at[k],
            device_id=(g, h, t, other), device_id_type=MESH,
        )
        for k, (src, dst) in enumerate([(g1, gall1), (g2, gall2)])
    ]
    for copy in gains:
        copy.start()

    def wait_in(kind, d, count):
        if T > 1 or not kind:
            pl.semaphore_wait(insem.at[kind, d], count)

    def upward(r, d):
        @pl.when(r < S - 1)
        def _():
            wait_in(0, d, C)
            for dc in range(C):
                send_stat((g, r, t, lax.rem(c + dc, C)))
            column_x(r)
            wait_in(1, d, (T - 1) * C)
            for dt in range(1, T):
                for dc in range(C):
                    send_stat((g, r, lax.rem(t + dt, T), lax.rem(c + dc, C)))

    rows_apart(1, upward)

    @pl.when(t < T - 1)
    def _():
        pl.semaphore_wait(insem.at[0, 0], (T - 1 - t) * C)
        pl.when(attends)(lambda: beside(1, send_stat))


    def last_in(r, d):
        @pl.when(r == S - 1)
        def _():
            wait_in(0, d, C)
            wait_in(1, d, (T - 1) * C)

    rows_apart(1, last_in)

    for copy in gains:
        copy.wait()
    population = float(n * W * GROUP)
    frame_at = t * C + c

    def attend(R):
        drain(stat1.at[pl.ds(0, n - 1)], s1sem)
        totals = jnp.sum(stat1[...].reshape(S * T, C, 2, half), axis=0)
        mean1, scale1 = moments(jnp.concatenate([totals[k] for k in range(C)], axis=1), population)
        factor1 = scale1 * jnp.concatenate([gall1[k] for k in range(C)], axis=1)

        def row_tokens(r):
            pieces = []
            for k in range(C):
                lanes = slice(k * half, (k + 1) * half)
                value = xall[r * C + k].astype(F32)
                pieces.append(((value - mean1[:, lanes]) * factor1[:, lanes]).astype(BF16))
            return jnp.concatenate(pieces, axis=1)

        def project(weight, first, stop):
            rows = tokens[first:stop].reshape((stop - first) * W, D)
            return jnp.dot(rows, weight[...], preferred_element_type=F32).astype(BF16)

        for dc in range(1, C):
            slot = h * C + lax.rem(c + dc, C)
            drain(xall.at[slot], xsem.at[slot])
        if R == 2:
            for k in range(C):
                slot = (h + 1) * C + k
                drain(xall.at[slot], xsem.at[slot])
        for i in range(R):
            tokens[i] = row_tokens(h + i)
        for load in loads[:3]:
            load.wait()
        queries = project(wq, 0, R)
        for i in range(S - R):
            r = i + jnp.where(i >= h, R, 0)
            for k in range(C):
                drain(xall.at[r * C + k], xsem.at[r * C + k])
        for i in range(S - R):
            tokens[R + i] = row_tokens(i + jnp.where(i >= h, R, 0))
        keyed[...] = project(wk, 0, S)
        valued[...] = project(wv, 0, S)

        scores = lax.dot_general(
            queries, keyed[...], (((1,), (1,)), ((), ())), preferred_element_type=F32
        ) * (D ** (-0.5))
        weights = jnp.exp(scores - jnp.max(scores, axis=1, keepdims=True))
        mass = jnp.sum(weights, axis=1, keepdims=True)
        mixed = jnp.dot(weights.astype(BF16), valued[...], preferred_element_type=F32)
        mixed = (mixed / mass).astype(BF16)
        loads[3].wait()
        attended = jnp.dot(mixed, wo[...], preferred_element_type=F32).astype(BF16)

        source = jnp.concatenate(
            [jnp.concatenate([xall[(h + i) * C + k] for k in range(C)], axis=1) for i in range(R)], axis=0
        ).astype(F32)
        resid = (source - mean1) + attended.astype(F32)
        sums, squares = channel_sums(resid)
        for k in range(T):
            lanes = slice(k * Kc, (k + 1) * Kc)
            stat2_src[k, 0:1] = sums[:, lanes]
            stat2_src[k, 1:2] = squares[:, lanes]

        def send_stat2(where):
            pltpu.make_async_remote_copy(
                src_ref=stat2_src.at[where[2]], dst_ref=stat2.at[me], send_sem=send_sem.at[4], recv_sem=s2sem,
                device_id=where, device_id_type=MESH,
            ).start()

        rows_apart(-1, lambda r, d: row_devices(r, send_stat2))
        rows_apart(1, lambda r, d: row_devices(r, send_stat2))
        beside(-1, send_stat2)
        beside(1, send_stat2)
        mates(send_stat2)
        for i in range(R):
            for k in range(T):
                dsrc[i, k] = resid[i * W : (i + 1) * W, k * Kc : (k + 1) * Kc].astype(BF16)
            for k in range(C):
                att_src[i, k] = attended[i * W : (i + 1) * W, k * half : (k + 1) * half]

        def send_row(i, r, cores, sends, recv):
            for dt in range(T):
                for dc in cores:
                    if not (r is h and dt == 0 and dc == 0):
                        to = lax.rem(t + dt, T)
                        pltpu.make_async_remote_copy(
                            src_ref=dsrc.at[i, to], dst_ref=dall.at[h + i - r + 1, frame_at],
                            send_sem=sends, recv_sem=recv,
                            device_id=(g, r, to, lax.rem(c + dc, C)), device_id_type=MESH,
                        ).start()

        everyone = range(C)
        if R == 2:
            for i in range(2):
                send_row(i, h + 1, [0], dsend.at[i], last_sem.at[i, t])

        @pl.when(h > 0)
        def _():
            send_row(0, h - 1, everyone, dsend.at[2], dsem.at[2])

        if R == 1:
            send_row(0, h + 1, everyone, dsend.at[3], dsem.at[0])
        for i in range(R):
            send_row(i, h, everyone, dsend.at[4 + i], dsem.at[1 + i])
            dall[1 + i, frame_at] = dsrc[i, t]
        attended_copy(0, other, h, other).start()
        if R == 2:
            for k in range(C):
                attended_copy(1, k, h + 1, k).start()
        stat2[me] = stat2_src[t]
        att_out[c, 0] = att_src[0, c]

    def attended_copy(i, k, r, core):
        return pltpu.make_async_remote_copy(
            src_ref=att_src.at[i, k], dst_ref=att_in.at[c], send_sem=asend.at[i * C + k], recv_sem=asem.at[c],
            device_id=(g, r, t, core), device_id_type=MESH,
        )

    def attended_in(frame):
        drain(att_in.at[frame], asem.at[frame])
        att_out[frame, 0] = att_in[frame]

    pl.when(h < S - 2)(lambda: attend(1))
    pl.when(h == S - 2)(lambda: attend(2))
    act[0:2] = jnp.zeros((2,) + act.shape[1:], BF16)
    gain2 = jnp.concatenate([gall2[k] for k in range(C)], axis=1)

    def share(i, k):
        return [
            pltpu.make_async_remote_copy(
                src_ref=dall.at[i, k * C + c], dst_ref=dall.at[i, k * C + c],
                send_sem=share_sem.at[i, k], recv_sem=dsem.at[i],
                device_id=(g, h, t, lax.rem(c + dc, C)), device_id_type=MESH,
            )
            for dc in range(1, C)
        ]

    @pl.when(jnp.logical_not(attends))
    def _():
        for dt in range(T):
            k = lax.rem(t + dt, T)
            for i in range(2):
                drain(dall.at[i, k * C + c], last_sem.at[i, k])
                for copy in share(i, k):
                    copy.start()
        drain(stat2.at[pl.ds(0, n - T * C)], s2sem)

    @pl.when(attends)
    def _():
        drain(stat2.at[pl.ds(0, n - T * C - 1)], s2sem)


    def sliced(v):
        out = v[:, 0:Kc]
        for k in range(1, T):
            out = jnp.where(t == k, v[:, k * Kc : (k + 1) * Kc], out)
        return out

    mean2, scale2 = slice_moments(jnp.sum(stat2[0 : n - T * C], axis=0), population)
    factor2 = scale2 * sliced(gain2)
    column = lax.broadcasted_iota(jnp.int32, (W, Kc), 0)

    def activate(row):
        @pl.loop(0, NF, unroll=NF <= 4)
        def _(f):
            v = (dall[row, f].astype(F32) - mean2) * factor2
            a = v / (1.0 + jnp.exp(-v))
            left = jnp.where(column == 0, 0.0, pltpu.roll(a, 1, 0))
            right = jnp.where(column == W - 1, 0.0, pltpu.roll(a, W - 1, 0))
            for e, piece in enumerate((left, a, right)):
                k = row * 3 + e
                act[f + 2, :, k * Kc : (k + 1) * Kc] = piece.astype(BF16)

    skips = (3 * Kc) % LANES == 0

    def blank(row):
        act[2:, :, row * 3 * Kc : (row + 1) * 3 * Kc] = jnp.zeros((NF, W, 3 * Kc), BF16)

    @pl.when(attends)
    def _():
        drain(dall.at[1, pl.ds(0, NF - 1)], dsem.at[1])

    @pl.when(jnp.logical_not(attends))
    def _():
        for i in range(2):
            drain(dall.at[i, pl.ds(0, (C - 1) * T)], dsem.at[i])

    activate(1)

    @pl.when(h > 0)
    def _():
        pl.when(attends)(lambda: drain(dall.at[0], dsem.at[0]))
        activate(0)

    @pl.when(attends)
    def _():
        pl.when(h < S - 2)(lambda: drain(dall.at[2], dsem.at[2]))
        pl.when(h == S - 2)(lambda: drain(dall.at[2, pl.ds(0, NF - 1)], dsem.at[2]))
        activate(2)

    if not skips:
        pl.when(h == 0)(lambda: blank(0))
        pl.when(h == S - 1)(lambda: blank(2))

    loads[4].wait()
    wide = half // CHUNKS

    def product(to, a0, b0, b1, chunk):
        total = None
        taps = slice(b0 * 3 * Kc, b1 * 3 * Kc)
        for a in range(a0, 3):
            window = act[pl.ds(to * C + a, C), :, taps].reshape(C * W, (b1 - b0) * 3 * Kc)
            weight = wc[a, taps, chunk * wide : (chunk + 1) * wide]
            term = jnp.dot(window, weight, preferred_element_type=F32)
            total = term if total is None else total + term
        return total

    if not skips:
        edges = [(t >= 0, 0, 3)]
    elif S == 1:
        edges = [(t >= 0, 1, 2)]
    else:
        edges = [(h == 0, 1, 3), (h == S - 1, 0, 2), (inner, 0, 3)]

    def partial(to, store):
        for at_edge, b0, b1 in edges:
            for early, a0 in ((to == 0, max(0, 3 - C)), (to > 0, 0)):

                @pl.when(at_edge & early)
                def _():
                    for chunk in range(CHUNKS):
                        store(chunk, product(to, a0, b0, b1, chunk))

    def part_copy(dt, chunk):
        return pltpu.make_async_remote_copy(
            src_ref=part_src.at[dt - 1, chunk], dst_ref=part.at[dt - 1, chunk],
            send_sem=psend.at[dt - 1, chunk], recv_sem=psem.at[dt - 1, chunk],
            device_id=(g, h, lax.rem(t + dt, T), c), device_id_type=MESH,
        )

    for dt in range(1, T):

        def send_part(chunk, value):
            part_src[dt - 1, chunk] = value.astype(BF16)
            part_copy(dt, chunk).start()

        partial(lax.rem(t + dt, T), send_part)


    def keep(chunk, value):
        own_total[chunk] = value

    partial(t, keep)
    attended_in(other)
    pl.when(jnp.logical_not(attends))(lambda: attended_in(c))

    for r in range(S - 1):

        @pl.when(h != r)
        def _():
            drain(stat1.at[pl.ds(0, T * C)], s1send.at[r])
            drain(xall.at[pl.ds(0, C)], xsend.at[r])

        @pl.when(h == r)
        def _():
            drain(stat1.at[pl.ds(0, T * C - 1)], s1send.at[r])
            drain(xall.at[pl.ds(0, C - 1)], xsend.at[r])

    @pl.when(attends)
    def _():
        drain(stat2.at[pl.ds(0, n - 1)], send_sem.at[4])
        drain(dall.at[1, pl.ds(0, NF - 1)], dsend.at[4])
        drain(att_src.at[0, 0], asend.at[other])

    @pl.when(attends & (h > 0))
    def _():
        drain(dall.at[0], dsend.at[2])

    @pl.when(h < S - 2)
    def _():
        drain(dall.at[0], dsend.at[3])

    @pl.when(h == S - 2)
    def _():
        drain(dall.at[1, pl.ds(0, NF - 1)], dsend.at[5])
        for i in range(2):
            drain(dall.at[0, pl.ds(0, T)], dsend.at[i])
        for k in range(C):
            drain(att_src.at[1, k], asend.at[C + k])

    @pl.when(jnp.logical_not(attends))
    def _():
        for i in range(2):
            for k in range(T):
                drain(dall.at[0, pl.ds(0, C - 1)], share_sem.at[i, k])

    for chunk in range(CHUNKS):
        total = own_total[chunk]
        for dt in range(1, T):
            part_copy(dt, chunk).wait()
            total = total + part[dt - 1, chunk].astype(F32)
        conv_out[:, 0, :, chunk * wide : (chunk + 1) * wide] = total.reshape(C, W, wide).astype(BF16)


def slice_moments(totals, population):
    Kc = totals.shape[1]
    if Kc >= LANES:
        return moments(totals, population)
    padded = jnp.concatenate([totals] * (LANES // Kc), axis=1)
    mean, scale = moments(padded, population)
    return mean[:, :Kc], scale[:, :Kc]


def hand_over(att_in, conv_in, att_out, conv_out):
    att_out[...] = att_in[...]
    conv_out[...] = conv_in[...]


def on_device(S, T, C, x, g1, g2, wq, wk, wv, wo, wc):
    frames, rows, W, half = x.shape
    assert frames == C and rows == 1 and half * C == D
    Kc = wc.shape[3]
    assert Kc * T == D and S > 1
    n, NF = S * T * C, T * C
    wide = half // CHUNKS
    wc = wc.reshape(3, 9 * Kc, half)
    vmem = pl.BlockSpec(memory_space=pltpu.VMEM)
    hbm = pl.BlockSpec(memory_space=pl.ANY)
    out = jax.ShapeDtypeStruct(x.shape, BF16)
    dma = pltpu.SemaphoreType.DMA
    kept = pltpu.VMEM(x.shape, BF16)
    links = max(T - 1, 1)
    results = pl.pallas_call(
        functools.partial(kernel, S, T, C, W),
        out_shape=(kept, kept),
        in_specs=[hbm] * 8,
        out_specs=(vmem, vmem),
        scratch_shapes=[
            pltpu.VMEM(x.shape, BF16),
            *[pltpu.VMEM((D, D), BF16)] * 4,
            pltpu.VMEM(wc.shape, BF16),
            pltpu.VMEM((2, half), F32),
            pltpu.VMEM((n, 2, half), F32),
            pltpu.VMEM((T, 2, Kc), F32),
            pltpu.VMEM((n, 2, Kc), F32),
            pltpu.VMEM((C, 1, half), F32),
            pltpu.VMEM((C, 1, half), F32),
            pltpu.VMEM((S * C, W, half), BF16),
            pltpu.VMEM((S, W, D), BF16),
            pltpu.VMEM((S * W, D), BF16),
            pltpu.VMEM((S * W, D), BF16),
            pltpu.VMEM((2, C, W, half), BF16),
            pltpu.VMEM((C, W, half), BF16),
            pltpu.VMEM((2, T, W, Kc), BF16),
            pltpu.VMEM((3, NF, W, Kc), BF16),
            pltpu.VMEM((NF + 2, W, 9 * Kc), BF16),
            pltpu.VMEM((CHUNKS, C * W, wide), F32),
            pltpu.VMEM((links, CHUNKS, C * W, wide), BF16),
            pltpu.VMEM((links, CHUNKS, C * W, wide), BF16),
            dma((3,)),
            dma((5,)),
            pltpu.SemaphoreType.REGULAR((2, S)),
            dma((5,)),
            dma((2,)),
            dma((S,)),
            dma(()),
            dma((S,)),
            dma((S * C,)),
            dma(()),
            dma((2 * C,)),
            dma((C,)),
            dma((6,)),
            dma((3,)),
            dma((2, T)),
            dma((2, T)),
            dma((links, CHUNKS)),
            dma((links, CHUNKS)),
        ],
        compiler_params=pltpu.CompilerParams(collective_id=0, has_side_effects=True),
    )(x, g1.reshape(1, half), g2.reshape(1, half), wq, wk, wv, wo, wc)
    return pl.pallas_call(
        hand_over, out_shape=(out, out), in_specs=[vmem] * 2, out_specs=(vmem, vmem),
    )(*[pltpu.with_memory_space_constraint(r, pltpu.VMEM) for r in results])


def solution(mesh):
    S, T, C = mesh.shape["space"], mesh.shape["tm"], mesh.shape["chan"]
    placed = (
        P(("groups", "tm"), "space", None, "chan"),
        P("chan"),
        P("chan"),
        P(),
        P(),
        P(),
        P(),
        P(None, None, None, "tm", "chan"),
    )
    return jax.shard_map(
        functools.partial(on_device, S, T, C),
        mesh=mesh,
        in_specs=placed,
        out_specs=(
            P(("groups", "tm"), "space", None, "chan"),
            P(("groups", "tm"), "space", None, "chan"),
        ),
        check_vma=False,
    )
```

time: 25.7 us -> 24.5 us (0.953)
  Pallas kernels: 24.9 us -> 23.7 us
    pallas_call x1, Pallas kernels: 24.3 us -> 23 us  [on_device(): pl.pallas_call(functools.partial(kernel, S, T, C, W), out_shape=(kept, ke...]
where the time goes in v1:
time: 24.5 us; the launch traced here: 24.3 us
  Pallas kernels  23.7 us (97%)
  between operations  0.64 us (3%)
    pallas_call x1, Pallas kernels, on_device(): pl.pallas_call(functools.partial(kernel, S, T, C, W), out_shape=(kept, ke...  23 us
    pallas_call x1, Pallas kernels, on_device(): pl.pallas_call(hand_over, out_shape=(out, out), in_specs=[vmem] * 2, out_...  0.66 us

profile of v1, /device:TPU:0, one launch (start us, length us, event | category | flops | bytes accessed | tf_op | source)
XLA Modules:
  0.0 24.3 jit_solution(14780130841085742757)
XLA Ops:
  0.6 23.0 %shard_map.95 = (bf16[2,1,64,256]{3,2,1,0:T(8,128)(2,1)S(1)}, bf16[2,1,64,256]{3,2,1,0:T(8,128)(2,1)S(1)}) custom-call(bf16[2,1,64,256]{3,2,1,0:T(8,128)(2,1)} %x_hbm.1, f32[1,256]{1,0:T(1,128)} %bitcast.4, f32[1,256]{1,0:T(1,128)} %bitcast.5, bf16[512,512]{1,0:T(8,128)(2,1)} %wq_hbm.1, bf16[512,512]{1,0:T(8,128)(2,1)} %wk_hbm.1, bf16[512,512]{1,0:T(8,128)(2,1)} %wv_hbm.1, ...), custom_call_target="tpu_custom_call" | custom-call | tf_op jit(solution)/shard_map/pallas_call | solution.py:543
  23.7 0.7 %shard_map.96 = (bf16[2,1,64,256]{3,2,1,0:T(8,128)(2,1)}, bf16[2,1,64,256]{3,2,1,0:T(8,128)(2,1)}) custom-call(bf16[2,1,64,256]{3,2,1,0:T(8,128)(2,1)S(1)} %get-tuple-element.4.att_in, bf16[2,1,64,256]{3,2,1,0:T(8,128)(2,1)S(1)} %get-tuple-element.5.conv_in), custom_call_target="tpu_custom_call" | custom-call | tf_op jit(solution)/shard_map/pallas_call | solution.py:591

commit v2 on v1

--- a/solution.py
+++ b/solution.py
@@ -50,24 +50,24 @@
     x_hbm, g1, g2, wq_hbm, wk_hbm, wv_hbm, wo_hbm, wc_hbm,
     att_out, conv_out,
     x, wq, wk, wv, wo, wc,
-    stat1_src, stat1, stat2_src, stat2, gall1, gall2,
+    stat1_src, row_sum, raw, last, stat1, tally, stat2_src, stat2, gall1, gall2,
     xall, tokens, keyed, valued, att_src, att_in, dsrc, dall, act, own_total, part_src, part,
-    xload, wsem, insem, send_sem, gsem, s1send, s1sem, xsend, xsem, s2sem,
-    asend, asem, dsend, dsem, last_sem, share_sem, psend, psem,
+    xload, wsem, insem, send_sem, gsem, raw_send, raw_sem, s1send, s1sem, xsend, xsem, s2sem,
+    asend, asem, dsend, dsem, outer_sem, share_sem, psend, psem,
 ):
     g = lax.axis_index("groups")
     h = lax.axis_index("space")
     t = lax.axis_index("tm")
     c = lax.axis_index("chan")
-    n = S * T * C
-    chip = h * T + t
-    me = chip * C + c
+    attending = (S - 2) * T * C
+    me = (h * T + t) * C + c - T * C
     half = D // C
     Kc = D // T
     NF = T * C
     other = lax.rem(c + 1, C)
-    inner = (h > 0) & (h < S - 1)
-    attends = h < S - 1
+    attends = (h > 0) & (h < S - 1)
+    at_edge = (h == 1) | (h == S - 2)
+    side = jnp.where(h == 1, -1, 1)
 
     def rows_apart(sign, act_on):
         def row(d):
@@ -82,12 +82,16 @@
             for dc in range(C):
                 act_on((g, r, lax.rem(t + dt, T), lax.rem(c + dc, C)))
 
-    def beside(sign, act_on):
+    def column(r, act_on):
+        for dc in range(C):
+            act_on((g, r, t, lax.rem(c + dc, C)))
+
+    def beside(sign, cores, act_on):
         for dt in range(1, T):
 
             @pl.when((t + sign * dt >= 0) & (t + sign * dt < T))
             def _():
-                for dc in range(C):
+                for dc in cores:
                     act_on((g, h, t + sign * dt, lax.rem(c + dc, C)))
 
     def mates(act_on):
@@ -100,6 +104,13 @@
     def drain(ref, sem):
         pltpu.make_async_copy(ref, ref, sem).wait()
 
+    def send(src, dst, sends, recvs, where):
+        copy = pltpu.make_async_remote_copy(
+            src_ref=src, dst_ref=dst, send_sem=sends, recv_sem=recvs, device_id=where, device_id_type=MESH,
+        )
+        copy.start()
+
+    everyone = range(C)
     first = [
         pltpu.make_async_copy(src, dst, xload.at[i])
         for i, (src, dst) in enumerate([(x_hbm, x), (g1, gall1.at[c]), (g2, gall2.at[c])])
@@ -108,17 +119,24 @@
         load.start()
     barrier = pltpu.get_barrier_semaphore()
     mates(signal(barrier))
-    beside(1, signal(barrier))
-    rows_apart(1, lambda r, d: row_devices(r, signal(barrier)))
-    pl.semaphore_wait(barrier, chip * C + C - 1)
-
-    def answer(r, d):
-        for dt in range(T):
-            for dc in range(C):
-                signal(insem.at[min(dt, 1), d])((g, r, lax.rem(t + dt, T), lax.rem(c + dc, C)))
-
-    rows_apart(-1, answer)
-    beside(-1, signal(insem.at[0, 0]))
+    pl.when(h < S - 1)(lambda: beside(1, [0], signal(barrier)))
+
+    def announce(r, d):
+        @pl.when(r == S - 1)
+        def _():
+            row_devices(r, signal(barrier))
+
+        @pl.when(r < S - 1)
+        def _():
+            column(r, signal(barrier))
+
+    rows_apart(1, announce)
+    pl.semaphore_wait(barrier, jnp.where(h == S - 1, (S - 1) * T * C, h * C + t) + C - 1)
+
+    @pl.when(h < S - 1)
+    def _():
+        rows_apart(-1, lambda r, d: column(r, signal(insem.at[d])))
+        beside(-1, [0], signal(insem.at[0]))
 
     loads = [
         pltpu.make_async_copy(src, dst, wsem.at[i])
@@ -126,7 +144,12 @@
             [(wk_hbm, wk), (wq_hbm, wq), (wv_hbm, wv), (wo_hbm, wo), (wc_hbm, wc)]
         )
     ]
-    pl.when(attends)(lambda: [load.start() for load in loads[:4]] and None)
+
+    @pl.when(attends)
+    def _():
+        for load in loads[:4]:
+            load.start()
+
     loads[4].start()
 
     for load in first:
@@ -134,36 +157,34 @@
     sums, squares = channel_sums(x[...].reshape(C * W, half).astype(F32))
     stat1_src[0:1] = sums
     stat1_src[1:2] = squares
-    stat1[me] = stat1_src[...]
-    xall[h * C + c] = x[c, 0]
-
-    def send_stat(where):
-        pltpu.make_async_remote_copy(
-            src_ref=stat1_src, dst_ref=stat1.at[me], send_sem=s1send.at[where[1]], recv_sem=s1sem,
-            device_id=where, device_id_type=MESH,
-        ).start()
 
     def send_x(r, dc):
         frame = lax.rem(c + dc, C)
-        pltpu.make_async_remote_copy(
-            src_ref=x.at[frame, 0], dst_ref=xall.at[h * C + c], send_sem=xsend.at[r], recv_sem=xsem.at[h * C + c],
-            device_id=(g, r, t, frame), device_id_type=MESH,
-        ).start()
+        slot = h * C + c
+        send(x.at[frame, 0], xall.at[slot], xsend.at[r], xsem.at[slot], (g, r, t, frame))
 
     def column_x(r):
         for dc in range(C):
             send_x(r, dc)
 
-    rows_apart(-1, lambda r, d: row_devices(r, send_stat))
+    def send_raw(where):
+        send(stat1_src, raw.at[t], raw_send, raw_sem.at[t], where)
+
+    @pl.when(h == S - 1)
+    def _():
+        for r in range(1, S - 1):
+            row_devices(r, lambda where: send(stat1_src, last.at[t, c], s1send.at[r], s1sem, where))
+
+    pl.when(h < S - 1)(lambda: beside(-1, [0], send_raw))
 
     @pl.when(attends)
     def _():
-        beside(-1, send_stat)
-        mates(send_stat)
+        xall[h * C + c] = x[c, 0]
         for dc in range(1, C):
             send_x(h, dc)
 
-    rows_apart(-1, lambda r, d: column_x(r))
+    for r in range(1, S - 1):
+        pl.when(r < h)(lambda: column_x(r))
 
     gains = [
         pltpu.make_async_remote_copy(
@@ -175,46 +196,67 @@
     for copy in gains:
         copy.start()
 
-    def wait_in(kind, d, count):
-        if T > 1 or not kind:
-            pl.semaphore_wait(insem.at[kind, d], count)
-
-    def upward(r, d):
-        @pl.when(r < S - 1)
-        def _():
-            wait_in(0, d, C)
-            for dc in range(C):
-                send_stat((g, r, t, lax.rem(c + dc, C)))
-            column_x(r)
-            wait_in(1, d, (T - 1) * C)
-            for dt in range(1, T):
-                for dc in range(C):
-                    send_stat((g, r, lax.rem(t + dt, T), lax.rem(c + dc, C)))
-
-    rows_apart(1, upward)
-
-    @pl.when(t < T - 1)
-    def _():
-        pl.semaphore_wait(insem.at[0, 0], (T - 1 - t) * C)
-        pl.when(attends)(lambda: beside(1, send_stat))
-
-
-    def last_in(r, d):
-        @pl.when(r == S - 1)
-        def _():
-            wait_in(0, d, C)
-            wait_in(1, d, (T - 1) * C)
-
-    rows_apart(1, last_in)
-
+    @pl.when(h < S - 2)
+    def _():
+        pl.semaphore_wait(insem.at[1], C)
+        column_x(h + 1)
+
+    @pl.when(h < S - 1)
+    def _():
+        @pl.when(t < T - 1)
+        def _():
+            pl.semaphore_wait(insem.at[0], T - 1 - t)
+            beside(1, [0], send_raw)
+
+        total = stat1_src[...]
+        for dt in range(1, T):
+            k = lax.rem(t + dt, T)
+            drain(raw.at[k], raw_sem.at[k])
+            total = total + raw[k]
+        row_sum[...] = total
+
+
+    def send_sum(where):
+        send(row_sum, stat1.at[h, c], s1send.at[where[1]], s1sem, where)
+
+    @pl.when(attends)
+    def _():
+        stat1[h, c] = row_sum[...]
+        mates(send_sum)
+        for r in range(1, S - 1):
+            pl.when(r < h)(lambda: column(r, send_sum))
+
+    pl.when(h < S - 2)(lambda: column(h + 1, send_sum))
+
+    def upward(d):
+        @pl.when(h + d < S - 1)
+        def _():
+            pl.semaphore_wait(insem.at[d], C)
+            column(h + d, send_sum)
+            column_x(h + d)
+
+    pl.loop(2, S - 1, unroll=S <= 4)(upward)
     for copy in gains:
         copy.wait()
-    population = float(n * W * GROUP)
+    population = float(S * T * C * W * GROUP)
     frame_at = t * C + c
 
+    def attended_copy(i, k, r, core):
+        return pltpu.make_async_remote_copy(
+            src_ref=att_src.at[i, k], dst_ref=att_in.at[c], send_sem=asend.at[i * C + k], recv_sem=asem.at[c],
+            device_id=(g, r, t, core), device_id_type=MESH,
+        )
+
     def attend(R):
-        drain(stat1.at[pl.ds(0, n - 1)], s1sem)
-        totals = jnp.sum(stat1[...].reshape(S * T, C, 2, half), axis=0)
+        outer = h + side
+        mine = [h, outer][:R]
+        skipped = jnp.where(h == 1, R, 0) if R == 2 else None
+
+        def rest(i):
+            return i + skipped if R == 2 else i + jnp.where(i >= h, 1, 0)
+
+        drain(tally, s1sem)
+        totals = jnp.sum(stat1[0 : S - 1], axis=0) + jnp.sum(last[...], axis=0)
         mean1, scale1 = moments(jnp.concatenate([totals[k] for k in range(C)], axis=1), population)
         factor1 = scale1 * jnp.concatenate([gall1[k] for k in range(C)], axis=1)
 
@@ -230,24 +272,24 @@
             rows = tokens[first:stop].reshape((stop - first) * W, D)
             return jnp.dot(rows, weight[...], preferred_element_type=F32).astype(BF16)
 
+        def slots_in(r):
+            for k in range(C):
+                drain(xall.at[r * C + k], xsem.at[r * C + k])
+
         for dc in range(1, C):
             slot = h * C + lax.rem(c + dc, C)
             drain(xall.at[slot], xsem.at[slot])
         if R == 2:
-            for k in range(C):
-                slot = (h + 1) * C + k
-                drain(xall.at[slot], xsem.at[slot])
+            slots_in(outer)
         for i in range(R):
-            tokens[i] = row_tokens(h + i)
+            tokens[i] = row_tokens(mine[i])
         for load in loads[:3]:
             load.wait()
         queries = project(wq, 0, R)
         for i in range(S - R):
-            r = i + jnp.where(i >= h, R, 0)
-            for k in range(C):
-                drain(xall.at[r * C + k], xsem.at[r * C + k])
+            slots_in(rest(i))
         for i in range(S - R):
-            tokens[R + i] = row_tokens(i + jnp.where(i >= h, R, 0))
+            tokens[R + i] = row_tokens(rest(i))
         keyed[...] = project(wk, 0, S)
         valued[...] = project(wv, 0, S)
 
@@ -262,7 +304,7 @@
         attended = jnp.dot(mixed, wo[...], preferred_element_type=F32).astype(BF16)
 
         source = jnp.concatenate(
-            [jnp.concatenate([xall[(h + i) * C + k] for k in range(C)], axis=1) for i in range(R)], axis=0
+            [jnp.concatenate([xall[r * C + k] for k in range(C)], axis=1) for r in mine], axis=0
         ).astype(F32)
         resid = (source - mean1) + attended.astype(F32)
         sums, squares = channel_sums(resid)
@@ -272,15 +314,12 @@
             stat2_src[k, 1:2] = squares[:, lanes]
 
         def send_stat2(where):
-            pltpu.make_async_remote_copy(
-                src_ref=stat2_src.at[where[2]], dst_ref=stat2.at[me], send_sem=send_sem.at[4], recv_sem=s2sem,
-                device_id=where, device_id_type=MESH,
-            ).start()
+            send(stat2_src.at[where[2]], stat2.at[me], send_sem.at[4], s2sem, where)
 
         rows_apart(-1, lambda r, d: row_devices(r, send_stat2))
         rows_apart(1, lambda r, d: row_devices(r, send_stat2))
-        beside(-1, send_stat2)
-        beside(1, send_stat2)
+        beside(-1, everyone, send_stat2)
+        beside(1, everyone, send_stat2)
         mates(send_stat2)
         for i in range(R):
             for k in range(T):
@@ -288,50 +327,40 @@
             for k in range(C):
                 att_src[i, k] = attended[i * W : (i + 1) * W, k * half : (k + 1) * half]
 
-        def send_row(i, r, cores, sends, recv):
+        def send_row(i, r, cores, sends, recv, skip_self=False):
             for dt in range(T):
                 for dc in cores:
-                    if not (r is h and dt == 0 and dc == 0):
+                    if not (skip_self and dt == 0 and dc == 0):
                         to = lax.rem(t + dt, T)
-                        pltpu.make_async_remote_copy(
-                            src_ref=dsrc.at[i, to], dst_ref=dall.at[h + i - r + 1, frame_at],
-                            send_sem=sends, recv_sem=recv,
-                            device_id=(g, r, to, lax.rem(c + dc, C)), device_id_type=MESH,
-                        ).start()
-
-        everyone = range(C)
+                        send(
+                            dsrc.at[i, to], dall.at[mine[i] - r + 1, frame_at], sends, recv,
+                            (g, r, to, lax.rem(c + dc, C)),
+                        )
+
         if R == 2:
             for i in range(2):
-                send_row(i, h + 1, [0], dsend.at[i], last_sem.at[i, t])
-
-        @pl.when(h > 0)
-        def _():
+                send_row(i, outer, [0], dsend.at[i], outer_sem.at[i, t])
+            send_row(0, h - side, everyone, dsend.at[2], dsem.at[1 + side])
+        else:
             send_row(0, h - 1, everyone, dsend.at[2], dsem.at[2])
-
-        if R == 1:
             send_row(0, h + 1, everyone, dsend.at[3], dsem.at[0])
         for i in range(R):
-            send_row(i, h, everyone, dsend.at[4 + i], dsem.at[1 + i])
-            dall[1 + i, frame_at] = dsrc[i, t]
+            send_row(i, h, everyone, dsend.at[4 + i], dsem.at[mine[i] - h + 1], skip_self=True)
+            dall[mine[i] - h + 1, frame_at] = dsrc[i, t]
         attended_copy(0, other, h, other).start()
         if R == 2:
             for k in range(C):
-                attended_copy(1, k, h + 1, k).start()
+                attended_copy(1, k, outer, k).start()
         stat2[me] = stat2_src[t]
         att_out[c, 0] = att_src[0, c]
-
-    def attended_copy(i, k, r, core):
-        return pltpu.make_async_remote_copy(
-            src_ref=att_src.at[i, k], dst_ref=att_in.at[c], send_sem=asend.at[i * C + k], recv_sem=asem.at[c],
-            device_id=(g, r, t, core), device_id_type=MESH,
-        )
 
     def attended_in(frame):
         drain(att_in.at[frame], asem.at[frame])
         att_out[frame, 0] = att_in[frame]
 
-    pl.when(h < S - 2)(lambda: attend(1))
-    pl.when(h == S - 2)(lambda: attend(2))
+    if S > 4:
+        pl.when(attends & jnp.logical_not(at_edge))(lambda: attend(1))
+    pl.when(at_edge)(lambda: attend(2))
     act[0:2] = jnp.zeros((2,) + act.shape[1:], BF16)
     gain2 = jnp.concatenate([gall2[k] for k in range(C)], axis=1)
 
@@ -345,19 +374,22 @@
             for dc in range(1, C)
         ]
 
+    beyond = jnp.where(h == 0, 1, 0)
+
     @pl.when(jnp.logical_not(attends))
     def _():
         for dt in range(T):
             k = lax.rem(t + dt, T)
             for i in range(2):
-                drain(dall.at[i, k * C + c], last_sem.at[i, k])
-                for copy in share(i, k):
+                row = beyond + i
+                drain(dall.at[row, k * C + c], outer_sem.at[jnp.where(h == 0, 1 - i, i), k])
+                for copy in share(row, k):
                     copy.start()
-        drain(stat2.at[pl.ds(0, n - T * C)], s2sem)
+        drain(stat2.at[pl.ds(0, attending)], s2sem)
 
     @pl.when(attends)
     def _():
-        drain(stat2.at[pl.ds(0, n - T * C - 1)], s2sem)
+        drain(stat2.at[pl.ds(0, attending - 1)], s2sem)
 
 
     def sliced(v):
@@ -366,7 +398,7 @@
             out = jnp.where(t == k, v[:, k * Kc : (k + 1) * Kc], out)
         return out
 
-    mean2, scale2 = slice_moments(jnp.sum(stat2[0 : n - T * C], axis=0), population)
+    mean2, scale2 = slice_moments(jnp.sum(stat2[0:attending], axis=0), population)
     factor2 = scale2 * sliced(gain2)
     column = lax.broadcasted_iota(jnp.int32, (W, Kc), 0)
 
@@ -392,21 +424,27 @@
 
     @pl.when(jnp.logical_not(attends))
     def _():
-        for i in range(2):
-            drain(dall.at[i, pl.ds(0, (C - 1) * T)], dsem.at[i])
+        drain(dall.at[1, pl.ds(0, (C - 1) * T)], dsem.at[1])
 
     activate(1)
 
-    @pl.when(h > 0)
-    def _():
-        pl.when(attends)(lambda: drain(dall.at[0], dsem.at[0]))
-        activate(0)
-
-    @pl.when(attends)
-    def _():
-        pl.when(h < S - 2)(lambda: drain(dall.at[2], dsem.at[2]))
-        pl.when(h == S - 2)(lambda: drain(dall.at[2, pl.ds(0, NF - 1)], dsem.at[2]))
-        activate(2)
+    def neighbour(row, edge, outermost):
+        @pl.when(edge)
+        def _():
+            drain(dall.at[row, pl.ds(0, NF - 1)], dsem.at[row])
+
+        @pl.when(outermost)
+        def _():
+            drain(dall.at[row, pl.ds(0, (C - 1) * T)], dsem.at[row])
+
+        @pl.when(jnp.logical_not(edge | outermost))
+        def _():
+            drain(dall.at[row], dsem.at[row])
+
+        activate(row)
+
+    pl.when(h > 0)(lambda: neighbour(0, h == 1, h == S - 1))
+    pl.when(h < S - 1)(lambda: neighbour(2, h == S - 2, h == 0))
 
     if not skips:
         pl.when(h == 0)(lambda: blank(0))
@@ -427,16 +465,14 @@
 
     if not skips:
         edges = [(t >= 0, 0, 3)]
-    elif S == 1:
-        edges = [(t >= 0, 1, 2)]
     else:
-        edges = [(h == 0, 1, 3), (h == S - 1, 0, 2), (inner, 0, 3)]
+        edges = [(h == 0, 1, 3), (h == S - 1, 0, 2), (attends, 0, 3)]
 
     def partial(to, store):
-        for at_edge, b0, b1 in edges:
+        for here, b0, b1 in edges:
             for early, a0 in ((to == 0, max(0, 3 - C)), (to > 0, 0)):
 
-                @pl.when(at_edge & early)
+                @pl.when(here & early)
                 def _():
                     for chunk in range(CHUNKS):
                         store(chunk, product(to, a0, b0, b1, chunk))
@@ -464,33 +500,40 @@
     attended_in(other)
     pl.when(jnp.logical_not(attends))(lambda: attended_in(c))
 
-    for r in range(S - 1):
-
-        @pl.when(h != r)
-        def _():
-            drain(stat1.at[pl.ds(0, T * C)], s1send.at[r])
+    @pl.when(h < S - 1)
+    def _():
+        if T > 1:
+            drain(raw.at[pl.ds(0, T - 1)], raw_send)
+
+    for r in range(1, S - 1):
+
+        @pl.when(h == S - 1)
+        def _():
+            drain(last.at[pl.ds(0, T)], s1send.at[r])
             drain(xall.at[pl.ds(0, C)], xsend.at[r])
 
+        @pl.when((h < S - 1) & (h != r))
+        def _():
+            drain(stat1.at[0], s1send.at[r])
+            drain(xall.at[pl.ds(0, C)], xsend.at[r])
+
         @pl.when(h == r)
         def _():
-            drain(stat1.at[pl.ds(0, T * C - 1)], s1send.at[r])
+            drain(stat1.at[0, pl.ds(0, C - 1)], s1send.at[r])
             drain(xall.at[pl.ds(0, C - 1)], xsend.at[r])
 
     @pl.when(attends)
     def _():
-        drain(stat2.at[pl.ds(0, n - 1)], send_sem.at[4])
+        drain(stat2.at[pl.ds(0, S * T * C - 1)], send_sem.at[4])
+        drain(dall.at[0], dsend.at[2])
         drain(dall.at[1, pl.ds(0, NF - 1)], dsend.at[4])
         drain(att_src.at[0, 0], asend.at[other])
 
-    @pl.when(attends & (h > 0))
-    def _():
-        drain(dall.at[0], dsend.at[2])
-
-    @pl.when(h < S - 2)
+    @pl.when(attends & jnp.logical_not(at_edge))
     def _():
         drain(dall.at[0], dsend.at[3])
 
-    @pl.when(h == S - 2)
+    @pl.when(at_edge)
     def _():
         drain(dall.at[1, pl.ds(0, NF - 1)], dsend.at[5])
         for i in range(2):
@@ -502,7 +545,7 @@
     def _():
         for i in range(2):
             for k in range(T):
-                drain(dall.at[0, pl.ds(0, C - 1)], share_sem.at[i, k])
+                drain(dall.at[0, pl.ds(0, C - 1)], share_sem.at[beyond + i, k])
 
     for chunk in range(CHUNKS):
         total = own_total[chunk]
@@ -530,7 +573,7 @@
     frames, rows, W, half = x.shape
     assert frames == C and rows == 1 and half * C == D
     Kc = wc.shape[3]
-    assert Kc * T == D and S > 1
+    assert Kc * T == D and S > 3
     n, NF = S * T * C, T * C
     wide = half // CHUNKS
     wc = wc.reshape(3, 9 * Kc, half)
@@ -550,7 +593,11 @@
             *[pltpu.VMEM((D, D), BF16)] * 4,
             pltpu.VMEM(wc.shape, BF16),
             pltpu.VMEM((2, half), F32),
-            pltpu.VMEM((n, 2, half), F32),
+            pltpu.VMEM((2, half), F32),
+            pltpu.VMEM((T, 2, half), F32),
+            pltpu.VMEM((T, C, 2, half), F32),
+            pltpu.VMEM((S - 1, C, 2, half), F32),
+            pltpu.VMEM(((S - 1 + T) * C - 1, 2, half), F32),
             pltpu.VMEM((T, 2, Kc), F32),
             pltpu.VMEM((n, 2, Kc), F32),
             pltpu.VMEM((C, 1, half), F32),
@@ -569,9 +616,11 @@
             pltpu.VMEM((links, CHUNKS, C * W, wide), BF16),
             dma((3,)),
             dma((5,)),
-            pltpu.SemaphoreType.REGULAR((2, S)),
+            pltpu.SemaphoreType.REGULAR((S,)),
             dma((5,)),
             dma((2,)),
+            dma(()),
+            dma((T,)),
             dma((S,)),
             dma(()),
             dma((S,)),
@@ -582,7 +631,7 @@
             dma((6,)),
             dma((3,)),
             dma((2, T)),
-            dma((2, T)),
+            dma((3, T)),
             dma((links, CHUNKS)),
             dma((links, CHUNKS)),
         ],

time: 24.5 us -> 23.7 us (0.967)
  Pallas kernels: 23.7 us -> 22.9 us
    pallas_call x1, Pallas kernels: 23 us -> 22.3 us  [on_device(): pl.pallas_call(functools.partial(kernel, S, T, C, W), out_shape=(kept, ke...]
where the time goes in v2:
time: 23.7 us; the launch traced here: 23.6 us
  Pallas kernels  22.9 us (97%)
  between operations  0.64 us (3%)
    pallas_call x1, Pallas kernels, on_device(): pl.pallas_call(functools.partial(kernel, S, T, C, W), out_shape=(kept, ke...  22.3 us
    pallas_call x1, Pallas kernels, on_device(): pl.pallas_call(hand_over, out_shape=(out, out), in_specs=[vmem] * 2, out_...  0.66 us

profile of v2, /device:TPU:0, one launch (start us, length us, event | category | flops | bytes accessed | tf_op | source)
XLA Modules:
  0.0 23.6 jit_solution(10646856608925586668)
XLA Ops:
  0.6 22.3 %shard_map.95 = (bf16[2,1,64,256]{3,2,1,0:T(8,128)(2,1)S(1)}, bf16[2,1,64,256]{3,2,1,0:T(8,128)(2,1)S(1)}) custom-call(bf16[2,1,64,256]{3,2,1,0:T(8,128)(2,1)} %x_hbm.1, f32[1,256]{1,0:T(1,128)} %bitcast.4, f32[1,256]{1,0:T(1,128)} %bitcast.5, bf16[512,512]{1,0:T(8,128)(2,1)} %wq_hbm.1, bf16[512,512]{1,0:T(8,128)(2,1)} %wk_hbm.1, bf16[512,512]{1,0:T(8,128)(2,1)} %wv_hbm.1, ...), custom_call_target="tpu_custom_call" | custom-call | tf_op jit(solution)/shard_map/pallas_call | solution.py:586
  22.9 0.7 %shard_map.96 = (bf16[2,1,64,256]{3,2,1,0:T(8,128)(2,1)}, bf16[2,1,64,256]{3,2,1,0:T(8,128)(2,1)}) custom-call(bf16[2,1,64,256]{3,2,1,0:T(8,128)(2,1)S(1)} %get-tuple-element.4.att_in, bf16[2,1,64,256]{3,2,1,0:T(8,128)(2,1)S(1)} %get-tuple-element.5.conv_in), custom_call_target="tpu_custom_call" | custom-call | tf_op jit(solution)/shard_map/pallas_call | solution.py:640

commit v3 on v2

v3 whole, which is shorter than its diff:
```python
import functools

import jax
import jax.numpy as jnp
from jax import lax
from jax.experimental import pallas as pl
from jax.experimental.pallas import tpu as pltpu
from jax.sharding import PartitionSpec as P

D = 512
NGROUP = 32
EPSILON = 1e-06
LANES = 128
CHUNKS = 2
GROUP = D // NGROUP
MESH = pl.DeviceIdType.MESH
F32 = jnp.float32
BF16 = jnp.bfloat16


def group_total(v):
    lane = lax.broadcasted_iota(jnp.int32, v.shape, 1)
    width = v.shape[1]
    step = 1
    while step < GROUP:
        above = pltpu.roll(v, width - step, 1)
        below = pltpu.roll(v, step, 1)
        v = v + jnp.where((lane // step) % 2 == 0, above, below)
        step *= 2
    return v


def channel_sums(values):
    return jnp.sum(values, axis=0, keepdims=True), jnp.sum(values * values, axis=0, keepdims=True)


def moments(totals, population):
    blocks = totals.shape[1] // LANES
    pieces = [totals[k : k + 1, b * LANES : (b + 1) * LANES] for k in range(2) for b in range(blocks)]
    rows = 8 * pl.cdiv(2 * blocks, 8)
    grouped = group_total(jnp.concatenate(pieces + pieces[:1] * (rows - 2 * blocks), axis=0)) / population
    mean = jnp.concatenate([grouped[b : b + 1] for b in range(blocks)], axis=1)
    square = jnp.concatenate([grouped[blocks + b : blocks + b + 1] for b in range(blocks)], axis=1)
    variance = jnp.maximum(square - mean * mean, 0.0)
    return mean, lax.rsqrt(variance + EPSILON)


def kernel(
    S, T, C, W,
    x_hbm, g1, g2, wq_hbm, wk_hbm, wv_hbm, wo_hbm, wc_hbm,
    att_out, conv_out,
    x, projections, wo, wc,
    stat1_src, stat1, stat2_src, stat2, gall,
    xall, tokens, keyed, valued, att_src, att_in, dsrc, dall, act, own_total, part_src, part,
    xload, wsem, insem, gsend, gsem, s1send, s1sem, xsend, xsem, s2send, s2sem,
    asend, asem, dsend, dsem, outer_sem, share_sem, psend, psem,
):
    g = lax.axis_index("groups")
    h = lax.axis_index("space")
    t = lax.axis_index("tm")
    c = lax.axis_index("chan")
    attending = (S - 2) * T * C
    me = (h * T + t) * C + c - T * C
    half = D // C
    Kc = D // T
    NF = T * C
    other = lax.rem(c + 1, C)
    attends = (h > 0) & (h < S - 1)
    at_edge = (h == 1) | (h == S - 2)
    side = jnp.where(h == 1, -1, 1)

    def rows_apart(sign, act_on):
        def row(d):
            @pl.when((h + sign * d >= 0) & (h + sign * d < S))
            def _():
                act_on(h + sign * d, d)

        pl.loop(1, S, unroll=S <= 4)(row)

    def row_devices(r, act_on):
        for dt in range(T):
            for dc in range(C):
                act_on((g, r, lax.rem(t + dt, T), lax.rem(c + dc, C)))

    def beside(sign, act_on):
        for dt in range(1, T):

            @pl.when((t + sign * dt >= 0) & (t + sign * dt < T))
            def _():
                for dc in range(C):
                    act_on((g, h, t + sign * dt, lax.rem(c + dc, C)))

    def mates(act_on):
        for dc in range(1, C):
            act_on((g, h, t, lax.rem(c + dc, C)))

    def signal(sem):
        return lambda where: pl.semaphore_signal(sem, inc=1, device_id=where, device_id_type=MESH)

    def drain(ref, sem):
        pltpu.make_async_copy(ref, ref, sem).wait()

    def send(src, dst, sends, recvs, where):
        copy = pltpu.make_async_remote_copy(
            src_ref=src, dst_ref=dst, send_sem=sends, recv_sem=recvs, device_id=where, device_id_type=MESH,
        )
        copy.start()

    everyone = range(C)
    x_load = pltpu.make_async_copy(x_hbm, x, xload.at[0])
    x_load.start()
    for k, gain in enumerate((g1, g2)):
        pltpu.make_async_copy(gain, gall.at[c, k], xload.at[1]).start()
    barrier = pltpu.get_barrier_semaphore()
    mates(signal(barrier))
    beside(1, signal(barrier))
    rows_apart(1, lambda r, d: row_devices(r, signal(barrier)))
    pl.semaphore_wait(barrier, (h * T + t) * C + C - 1)

    def answer(r, d):
        for dt in range(T):
            for dc in range(C):
                signal(insem.at[min(dt, 1), d])((g, r, lax.rem(t + dt, T), lax.rem(c + dc, C)))

    @pl.when(h < S - 1)
    def _():
        rows_apart(-1, answer)
        pl.when(h > 0)(lambda: beside(-1, signal(insem.at[0, 0])))

    loads = [
        pltpu.make_async_copy(src, dst, wsem.at[i])
        for i, (src, dst) in zip((0, 0, 0, 1, 2), [(wq_hbm, projections.at[0]), (wk_hbm, projections.at[1]), (wv_hbm, projections.at[2]), (wo_hbm, wo), (wc_hbm, wc)])
    ]

    @pl.when(attends)
    def _():
        for load in loads[:4]:
            load.start()

    loads[4].start()

    x_load.wait()
    sums, squares = channel_sums(x[...].reshape(C * W, half).astype(F32))
    stat1_src[0:1] = sums
    stat1_src[1:2] = squares
    at = (h * T + t) * C + c

    def send_stat(where):
        send(stat1_src, stat1.at[at], s1send, s1sem, where)

    def send_x(r, dc):
        frame = lax.rem(c + dc, C)
        send(x.at[frame, 0], xall.at[h * C + c], xsend, xsem.at[h], (g, r, t, frame))

    def column_x(r):
        for dc in range(C):
            send_x(r, dc)

    for r in range(1, S - 1):
        pl.when(r < h)(lambda: row_devices(r, send_stat))

    @pl.when(attends)
    def _():
        stat1[at] = stat1_src[...]
        beside(-1, send_stat)
        mates(send_stat)
        xall[h * C + c] = x[c, 0]
        for dc in range(1, C):
            send_x(h, dc)

    for r in range(1, S - 1):
        pl.when(r < h)(lambda: column_x(r))

    drain(gall.at[c], xload.at[1])
    mates(lambda where: send(gall.at[c], gall.at[c], gsend, gsem, where))

    def upward(r, d):
        @pl.when(r < S - 1)
        def _():
            pl.semaphore_wait(insem.at[0, d], C)
            for dc in range(C):
                send_stat((g, r, t, lax.rem(c + dc, C)))
            column_x(r)
            if T > 1:
                pl.semaphore_wait(insem.at[1, d], (T - 1) * C)
            for dt in range(1, T):
                for dc in range(C):
                    send_stat((g, r, lax.rem(t + dt, T), lax.rem(c + dc, C)))

    @pl.when(attends & (t < T - 1))
    def _():
        pl.semaphore_wait(insem.at[0, 0], (T - 1 - t) * C)
        beside(1, send_stat)

    rows_apart(1, upward)
    drain(gall.at[pl.ds(0, C - 1)], gsem)
    population = float(S * T * C * W * GROUP)
    frame_at = t * C + c

    def send_attended(i, k, r, core):
        send(att_src.at[i, k], att_in.at[c], asend, asem, (g, r, t, core))

    def attend(R):
        outer = h + side
        mine = [h, outer][:R]
        skipped = jnp.where(h == 1, R, 0) if R == 2 else None

        def rest(i):
            return i + skipped if R == 2 else i + jnp.where(i >= h, 1, 0)

        drain(stat1.at[pl.ds(0, S * T * C - 1)], s1sem)
        totals = jnp.sum(stat1[...].reshape(S * T, C, 2, half), axis=0)
        mean1, scale1 = moments(jnp.concatenate([totals[k] for k in range(C)], axis=1), population)
        factor1 = scale1 * jnp.concatenate([gall[k, 0] for k in range(C)], axis=1)

        def row_tokens(r):
            pieces = []
            for k in range(C):
                lanes = slice(k * half, (k + 1) * half)
                value = xall[r * C + k].astype(F32)
                pieces.append(((value - mean1[:, lanes]) * factor1[:, lanes]).astype(BF16))
            return jnp.concatenate(pieces, axis=1)

        def project(weight, first, stop):
            rows = tokens[first:stop].reshape((stop - first) * W, D)
            return jnp.dot(rows, weight[...], preferred_element_type=F32).astype(BF16)

        def slots_in(r):
            drain(xall.at[pl.ds(r * C, C)], xsem.at[r])

        drain(xall.at[pl.ds(0, C - 1)], xsem.at[h])
        if R == 2:
            slots_in(outer)
        for i in range(R):
            tokens[i] = row_tokens(mine[i])
        drain(projections, wsem.at[0])
        queries = project(projections.at[0], 0, R)
        for i in range(S - R):
            slots_in(rest(i))
        for i in range(S - R):
            tokens[R + i] = row_tokens(rest(i))
        keyed[...] = project(projections.at[1], 0, S)
        valued[...] = project(projections.at[2], 0, S)

        scores = lax.dot_general(
            queries, keyed[...], (((1,), (1,)), ((), ())), preferred_element_type=F32
        ) * (D ** (-0.5))
        weights = jnp.exp(scores - jnp.max(scores, axis=1, keepdims=True))
        mass = jnp.sum(weights, axis=1, keepdims=True)
        mixed = jnp.dot(weights.astype(BF16), valued[...], preferred_element_type=F32)
        mixed = (mixed / mass).astype(BF16)
        loads[3].wait()
        attended = jnp.dot(mixed, wo[...], preferred_element_type=F32).astype(BF16)

        source = jnp.concatenate(
            [jnp.concatenate([xall[r * C + k] for k in range(C)], axis=1) for r in mine], axis=0
        ).astype(F32)
        resid = (source - mean1) + attended.astype(F32)
        for i in range(R):
            for k in range(T):
                dsrc[i, k] = resid[i * W : (i + 1) * W, k * Kc : (k + 1) * Kc].astype(BF16)

        def send_row(i, r, cores, sends, recv, skip_self=False):
            for dt in range(T):
                for dc in cores:
                    if not (skip_self and dt == 0 and dc == 0):
                        to = lax.rem(t + dt, T)
                        send(
                            dsrc.at[i, to], dall.at[(mine[i] - r + 1) * NF + frame_at], sends, recv,
                            (g, r, to, lax.rem(c + dc, C)),
                        )

        if R == 2:
            for i in range(2):
                send_row(i, outer, [0], dsend.at[0], outer_sem.at[i, t])
        sums, squares = channel_sums(resid)
        for k in range(T):
            lanes = slice(k * Kc, (k + 1) * Kc)
            stat2_src[k, 0:1] = sums[:, lanes]
            stat2_src[k, 1:2] = squares[:, lanes]

        def send_stat2(where):
            send(stat2_src.at[where[2]], stat2.at[me], s2send, s2sem, where)

        rows_apart(-1, lambda r, d: row_devices(r, send_stat2))
        rows_apart(1, lambda r, d: row_devices(r, send_stat2))
        beside(-1, send_stat2)
        beside(1, send_stat2)
        mates(send_stat2)
        if R == 2:
            send_row(0, h - side, everyone, dsend.at[1], dsem.at[1 + side])
        else:
            send_row(0, h - 1, everyone, dsend.at[1], dsem.at[2])
            send_row(0, h + 1, everyone, dsend.at[1], dsem.at[0])
        for i in range(R):
            row = mine[i] - h + 1
            send_row(i, h, everyone, dsend.at[1], dsem.at[row], skip_self=True)
            dall[row * NF + frame_at] = dsrc[i, t]
        for i in range(R):
            for k in range(C):
                att_src[i, k] = attended[i * W : (i + 1) * W, k * half : (k + 1) * half]
        send_attended(0, other, h, other)
        if R == 2:
            for k in range(C):
                send_attended(1, k, outer, k)
        stat2[me] = stat2_src[t]
        att_out[c, 0] = att_src[0, c]

    if S > 4:
        pl.when(attends & jnp.logical_not(at_edge))(lambda: attend(1))
    pl.when(at_edge)(lambda: attend(2))
    act[0:2] = jnp.zeros((2,) + act.shape[1:], BF16)
    gain2 = jnp.concatenate([gall[k, 1] for k in range(C)], axis=1)

    beyond = jnp.where(h == 0, 1, 0)

    @pl.when(jnp.logical_not(attends))
    def _():
        for dt in range(T):
            k = lax.rem(t + dt, T)
            for i in range(2):
                row = beyond + i
                slot = row * NF + k * C + c
                drain(dall.at[slot], outer_sem.at[jnp.where(h == 0, 1 - i, i), k])
                mates(lambda where: send(dall.at[slot], dall.at[slot], share_sem, dsem.at[row], where))
        drain(stat2.at[pl.ds(0, attending)], s2sem)

    @pl.when(attends)
    def _():
        drain(stat2.at[pl.ds(0, attending - 1)], s2sem)


    def sliced(v):
        out = v[:, 0:Kc]
        for k in range(1, T):
            out = jnp.where(t == k, v[:, k * Kc : (k + 1) * Kc], out)
        return out

    mean2, scale2 = slice_moments(jnp.sum(stat2[0:attending], axis=0), population)
    factor2 = scale2 * sliced(gain2)
    column = lax.broadcasted_iota(jnp.int32, (W, Kc), 0)

    def activate(row):
        @pl.loop(0, NF, unroll=NF <= 4)
        def _(f):
            v = (dall[row * NF + f].astype(F32) - mean2) * factor2
            a = v / (1.0 + jnp.exp(-v))
            left = jnp.where(column == 0, 0.0, pltpu.roll(a, 1, 0))
            right = jnp.where(column == W - 1, 0.0, pltpu.roll(a, W - 1, 0))
            for e, piece in enumerate((left, a, right)):
                k = row * 3 + e
                act[f + 2, :, k * Kc : (k + 1) * Kc] = piece.astype(BF16)

    skips = (3 * Kc) % LANES == 0

    def blank(row):
        act[2:, :, row * 3 * Kc : (row + 1) * 3 * Kc] = jnp.zeros((NF, W, 3 * Kc), BF16)

    @pl.when(attends)
    def _():
        drain(dall.at[pl.ds(0, NF - 1)], dsem.at[1])

    @pl.when(jnp.logical_not(attends))
    def _():
        drain(dall.at[pl.ds(0, (C - 1) * T)], dsem.at[1])

    activate(1)

    def neighbour(row, edge, outermost):
        @pl.when(edge)
        def _():
            drain(dall.at[pl.ds(0, NF - 1)], dsem.at[row])

        @pl.when(outermost)
        def _():
            drain(dall.at[pl.ds(0, (C - 1) * T)], dsem.at[row])

        @pl.when(jnp.logical_not(edge | outermost))
        def _():
            drain(dall.at[pl.ds(0, NF)], dsem.at[row])

        activate(row)

    pl.when(h > 0)(lambda: neighbour(0, h == 1, h == S - 1))
    pl.when(h < S - 1)(lambda: neighbour(2, h == S - 2, h == 0))

    if not skips:
        pl.when(h == 0)(lambda: blank(0))
        pl.when(h == S - 1)(lambda: blank(2))

    loads[4].wait()
    wide = half // CHUNKS

    def product(to, a0, b0, b1, chunk):
        total = None
        taps = slice(b0 * 3 * Kc, b1 * 3 * Kc)
        for a in range(a0, 3):
            window = act[pl.ds(to * C + a, C), :, taps].reshape(C * W, (b1 - b0) * 3 * Kc)
            weight = wc[a, taps, chunk * wide : (chunk + 1) * wide]
            term = jnp.dot(window, weight, preferred_element_type=F32)
            total = term if total is None else total + term
        return total

    if not skips:
        edges = [(t >= 0, 0, 3)]
    else:
        edges = [(h == 0, 1, 3), (h == S - 1, 0, 2), (attends, 0, 3)]

    def partial(to, store):
        for here, b0, b1 in edges:
            for early, a0 in ((to == 0, max(0, 3 - C)), (to > 0, 0)):

                @pl.when(here & early)
                def _():
                    for chunk in range(CHUNKS):
                        store(chunk, product(to, a0, b0, b1, chunk))

    for dt in range(1, T):

        def send_part(chunk, value):
            part_src[dt - 1, chunk] = value.astype(BF16)
            send(
                part_src.at[dt - 1, chunk], part.at[dt - 1, chunk], psend, psem.at[dt - 1, chunk],
                (g, h, lax.rem(t + dt, T), c),
            )

        partial(lax.rem(t + dt, T), send_part)


    def keep(chunk, value):
        own_total[chunk] = value

    partial(t, keep)
    @pl.when(attends)
    def _():
        drain(att_in.at[pl.ds(0, C - 1)], asem)
        att_out[other, 0] = att_in[other]
        drain(stat1.at[pl.ds(0, attending - 1)], s1send)
        drain(xall.at[pl.ds(0, (S - 2) * C - 1)], xsend)
        drain(stat2.at[pl.ds(0, S * T * C - 1)], s2send)

    @pl.when(jnp.logical_not(attends))
    def _():
        drain(att_in, asem)
        for k in range(C):
            att_out[k, 0] = att_in[k]
        drain(stat1.at[pl.ds(0, attending)], s1send)
        drain(xall.at[pl.ds(0, (S - 2) * C)], xsend)
        drain(dall.at[pl.ds(0, 2 * T * (C - 1))], share_sem)

    @pl.when(attends & jnp.logical_not(at_edge))
    def _():
        drain(dall.at[pl.ds(0, 3 * NF - 1)], dsend.at[1])
        drain(att_src.at[0, 0], asend)

    @pl.when(at_edge)
    def _():
        drain(dall.at[pl.ds(0, 2 * T)], dsend.at[0])
        drain(dall.at[pl.ds(0, 3 * NF - 2)], dsend.at[1])
        drain(xall.at[pl.ds(0, C + 1)], asend)

    drain(gall.at[pl.ds(0, C - 1)], gsend)
    for chunk in range(CHUNKS):
        total = own_total[chunk]
        for dt in range(1, T):
            drain(part.at[dt - 1, chunk], psem.at[dt - 1, chunk])
            total = total + part[dt - 1, chunk].astype(F32)
        conv_out[:, 0, :, chunk * wide : (chunk + 1) * wide] = total.reshape(C, W, wide).astype(BF16)
    if T > 1:
        drain(part_src, psend)


def slice_moments(totals, population):
    Kc = totals.shape[1]
    if Kc >= LANES:
        return moments(totals, population)
    padded = jnp.concatenate([totals] * (LANES // Kc), axis=1)
    mean, scale = moments(padded, population)
    return mean[:, :Kc], scale[:, :Kc]


def hand_over(att_in, conv_in, att_out, conv_out):
    att_out[...] = att_in[...]
    conv_out[...] = conv_in[...]


def on_device(S, T, C, x, g1, g2, wq, wk, wv, wo, wc):
    frames, rows, W, half = x.shape
    assert frames == C and rows == 1 and half * C == D
    Kc = wc.shape[3]
    assert Kc * T == D and S > 3
    n, NF = S * T * C, T * C
    wide = half // CHUNKS
    wc = wc.reshape(3, 9 * Kc, half)
    vmem = pl.BlockSpec(memory_space=pltpu.VMEM)
    hbm = pl.BlockSpec(memory_space=pl.ANY)
    out = jax.ShapeDtypeStruct(x.shape, BF16)
    dma = pltpu.SemaphoreType.DMA
    kept = pltpu.VMEM(x.shape, BF16)
    links = max(T - 1, 1)
    results = pl.pallas_call(
        functools.partial(kernel, S, T, C, W),
        out_shape=(kept, kept),
        in_specs=[hbm] * 8,
        out_specs=(vmem, vmem),
        scratch_shapes=[
            pltpu.VMEM(x.shape, BF16),
            pltpu.VMEM((3, D, D), BF16),
            pltpu.VMEM((D, D), BF16),
            pltpu.VMEM(wc.shape, BF16),
            pltpu.VMEM((2, half), F32),
            pltpu.VMEM((n, 2, half), F32),
            pltpu.VMEM((T, 2, Kc), F32),
            pltpu.VMEM((n, 2, Kc), F32),
            pltpu.VMEM((C, 2, 1, half), F32),
            pltpu.VMEM((S * C, W, half), BF16),
            pltpu.VMEM((S, W, D), BF16),
            pltpu.VMEM((S * W, D), BF16),
            pltpu.VMEM((S * W, D), BF16),
            pltpu.VMEM((2, C, W, half), BF16),
            pltpu.VMEM((C, W, half), BF16),
            pltpu.VMEM((2, T, W, Kc), BF16),
            pltpu.VMEM((3 * NF, W, Kc), BF16),
            pltpu.VMEM((NF + 2, W, 9 * Kc), BF16),
            pltpu.VMEM((CHUNKS, C * W, wide), F32),
            pltpu.VMEM((links, CHUNKS, C * W, wide), BF16),
            pltpu.VMEM((links, CHUNKS, C * W, wide), BF16),
            dma((2,)),
            dma((3,)),
            pltpu.SemaphoreType.REGULAR((2, S - 1)),
            dma(()),
            dma(()),
            dma(()),
            dma(()),
            dma(()),
            dma((S,)),
            dma(()),
            dma(()),
            dma(()),
            dma(()),
            dma((2,)),
            dma((3,)),
            dma((2, T)),
            dma(()),
            dma(()),
            dma((links, CHUNKS)),
        ],
        compiler_params=pltpu.CompilerParams(collective_id=0, has_side_effects=True),
    )(x, g1.reshape(1, half), g2.reshape(1, half), wq, wk, wv, wo, wc)
    return pl.pallas_call(
        hand_over, out_shape=(out, out), in_specs=[vmem] * 2, out_specs=(vmem, vmem),
    )(*[pltpu.with_memory_space_constraint(r, pltpu.VMEM) for r in results])


def solution(mesh):
    S, T, C = mesh.shape["space"], mesh.shape["tm"], mesh.shape["chan"]
    placed = (
        P(("groups", "tm"), "space", None, "chan"),
        P("chan"),
        P("chan"),
        P(),
        P(),
        P(),
        P(),
        P(None, None, None, "tm", "chan"),
    )
    return jax.shard_map(
        functools.partial(on_device, S, T, C),
        mesh=mesh,
        in_specs=placed,
        out_specs=(
            P(("groups", "tm"), "space", None, "chan"),
            P(("groups", "tm"), "space", None, "chan"),
        ),
        check_vma=False,
    )
```

time: 23.7 us -> 23 us (0.970)
  Pallas kernels: 22.9 us -> 22.2 us
    pallas_call x1, Pallas kernels: 22.3 us -> 21.6 us  [on_device(): pl.pallas_call(functools.partial(kernel, S, T, C, W), out_shape=(kept, ke...]
where the time goes in v3:
time: 23 us; the launch traced here: 22.9 us
  Pallas kernels  22.2 us (97%)
  between operations  0.64 us (3%)
    pallas_call x1, Pallas kernels, on_device(): pl.pallas_call(functools.partial(kernel, S, T, C, W), out_shape=(kept, ke...  21.6 us
    pallas_call x1, Pallas kernels, on_device(): pl.pallas_call(hand_over, out_shape=(out, out), in_specs=[vmem] * 2, out_...  0.66 us

profile of v3, /device:TPU:0, one launch (start us, length us, event | category | flops | bytes accessed | tf_op | source)
XLA Modules:
  0.0 22.9 jit_solution(15592432603166661269)
XLA Ops:
  0.6 21.6 %shard_map.95 = (bf16[2,1,64,256]{3,2,1,0:T(8,128)(2,1)S(1)}, bf16[2,1,64,256]{3,2,1,0:T(8,128)(2,1)S(1)}) custom-call(bf16[2,1,64,256]{3,2,1,0:T(8,128)(2,1)} %x_hbm.1, f32[1,256]{1,0:T(1,128)} %bitcast.4, f32[1,256]{1,0:T(1,128)} %bitcast.5, bf16[512,512]{1,0:T(8,128)(2,1)} %wq_hbm.1, bf16[512,512]{1,0:T(8,128)(2,1)} %wk_hbm.1, bf16[512,512]{1,0:T(8,128)(2,1)} %wv_hbm.1, ...), custom_call_target="tpu_custom_call" | custom-call | tf_op jit(solution)/shard_map/pallas_call | solution.py:501
  22.2 0.7 %shard_map.96 = (bf16[2,1,64,256]{3,2,1,0:T(8,128)(2,1)}, bf16[2,1,64,256]{3,2,1,0:T(8,128)(2,1)}) custom-call(bf16[2,1,64,256]{3,2,1,0:T(8,128)(2,1)S(1)} %get-tuple-element.4.att_in, bf16[2,1,64,256]{3,2,1,0:T(8,128)(2,1)S(1)} %get-tuple-element.5.conv_in), custom_call_target="tpu_custom_call" | custom-call | tf_op jit(solution)/shard_map/pallas_call | solution.py:550

commit v4 on v3

--- a/solution.py
+++ b/solution.py
@@ -113,9 +113,9 @@
         pltpu.make_async_copy(gain, gall.at[c, k], xload.at[1]).start()
     barrier = pltpu.get_barrier_semaphore()
     mates(signal(barrier))
-    beside(1, signal(barrier))
+    pl.when(attends)(lambda: beside(-1, signal(barrier)))
     rows_apart(1, lambda r, d: row_devices(r, signal(barrier)))
-    pl.semaphore_wait(barrier, (h * T + t) * C + C - 1)
+    pl.semaphore_wait(barrier, (h * T + jnp.where(attends, T - 1 - t, 0)) * C + C - 1)
 
     def answer(r, d):
         for dt in range(T):
@@ -125,7 +125,7 @@
     @pl.when(h < S - 1)
     def _():
         rows_apart(-1, answer)
-        pl.when(h > 0)(lambda: beside(-1, signal(insem.at[0, 0])))
+        pl.when(h > 0)(lambda: beside(1, signal(insem.at[0, 0])))
 
     loads = [
         pltpu.make_async_copy(src, dst, wsem.at[i])
@@ -162,7 +162,7 @@
     @pl.when(attends)
     def _():
         stat1[at] = stat1_src[...]
-        beside(-1, send_stat)
+        beside(1, send_stat)
         mates(send_stat)
         xall[h * C + c] = x[c, 0]
         for dc in range(1, C):
@@ -187,12 +187,13 @@
                 for dc in range(C):
                     send_stat((g, r, lax.rem(t + dt, T), lax.rem(c + dc, C)))
 
-    @pl.when(attends & (t < T - 1))
-    def _():
-        pl.semaphore_wait(insem.at[0, 0], (T - 1 - t) * C)
-        beside(1, send_stat)
-
     rows_apart(1, upward)
+
+    @pl.when(attends & (t > 0))
+    def _():
+        pl.semaphore_wait(insem.at[0, 0], t * C)
+        beside(-1, send_stat)
+
     drain(gall.at[pl.ds(0, C - 1)], gsem)
     population = float(S * T * C * W * GROUP)
     frame_at = t * C + c
@@ -260,8 +261,8 @@
             for k in range(T):
                 dsrc[i, k] = resid[i * W : (i + 1) * W, k * Kc : (k + 1) * Kc].astype(BF16)
 
-        def send_row(i, r, cores, sends, recv, skip_self=False):
-            for dt in range(T):
+        def send_row(i, r, cores, sends, recv, skip_self=False, own=None):
+            for dt in {None: [*range(1, T), 0], False: range(1, T), True: [0]}[own]:
                 for dc in cores:
                     if not (skip_self and dt == 0 and dc == 0):
                         to = lax.rem(t + dt, T)
@@ -271,8 +272,9 @@
                         )
 
         if R == 2:
-            for i in range(2):
-                send_row(i, outer, [0], dsend.at[0], outer_sem.at[i, t])
+            for own in (False, True):
+                for i in range(2):
+                    send_row(i, outer, [0], dsend.at[0], outer_sem.at[i, t], own=own)
         sums, squares = channel_sums(resid)
         for k in range(T):
             lanes = slice(k * Kc, (k + 1) * Kc)
@@ -288,13 +290,13 @@
         beside(1, send_stat2)
         mates(send_stat2)
         if R == 2:
-            send_row(0, h - side, everyone, dsend.at[1], dsem.at[1 + side])
+            send_row(0, h - side, everyone, dsend.at[1], dsem.at[1 + side, t])
         else:
-            send_row(0, h - 1, everyone, dsend.at[1], dsem.at[2])
-            send_row(0, h + 1, everyone, dsend.at[1], dsem.at[0])
+            send_row(0, h - 1, everyone, dsend.at[1], dsem.at[2, t])
+            send_row(0, h + 1, everyone, dsend.at[1], dsem.at[0, t])
         for i in range(R):
             row = mine[i] - h + 1
-            send_row(i, h, everyone, dsend.at[1], dsem.at[row], skip_self=True)
+            send_row(i, h, everyone, dsend.at[1], dsem.at[row, t], skip_self=True)
             dall[row * NF + frame_at] = dsrc[i, t]
         for i in range(R):
             for k in range(C):
@@ -314,15 +316,18 @@
 
     beyond = jnp.where(h == 0, 1, 0)
 
+    def forward(k):
+        for i in range(2):
+            row = beyond + i
+            slot = row * NF + k * C + c
+            drain(dall.at[slot], outer_sem.at[jnp.where(h == 0, 1 - i, i), k])
+            mates(lambda where: send(dall.at[slot], dall.at[slot], share_sem, dsem.at[row, k], where))
+
     @pl.when(jnp.logical_not(attends))
     def _():
-        for dt in range(T):
-            k = lax.rem(t + dt, T)
-            for i in range(2):
-                row = beyond + i
-                slot = row * NF + k * C + c
-                drain(dall.at[slot], outer_sem.at[jnp.where(h == 0, 1 - i, i), k])
-                mates(lambda where: send(dall.at[slot], dall.at[slot], share_sem, dsem.at[row], where))
+        forward(0)
+        for k in range(1, T):
+            pl.when(t < k)(lambda: forward(k))
         drain(stat2.at[pl.ds(0, attending)], s2sem)
 
     @pl.when(attends)
@@ -340,62 +345,52 @@
     factor2 = scale2 * sliced(gain2)
     column = lax.broadcasted_iota(jnp.int32, (W, Kc), 0)
 
-    def activate(row):
-        @pl.loop(0, NF, unroll=NF <= 4)
-        def _(f):
+    def activate(row, k):
+        for f in range(k * C, (k + 1) * C):
             v = (dall[row * NF + f].astype(F32) - mean2) * factor2
             a = v / (1.0 + jnp.exp(-v))
             left = jnp.where(column == 0, 0.0, pltpu.roll(a, 1, 0))
             right = jnp.where(column == W - 1, 0.0, pltpu.roll(a, W - 1, 0))
             for e, piece in enumerate((left, a, right)):
-                k = row * 3 + e
-                act[f + 2, :, k * Kc : (k + 1) * Kc] = piece.astype(BF16)
+                place = row * 3 + e
+                act[f + 2, :, place * Kc : (place + 1) * Kc] = piece.astype(BF16)
 
     skips = (3 * Kc) % LANES == 0
 
     def blank(row):
         act[2:, :, row * 3 * Kc : (row + 1) * 3 * Kc] = jnp.zeros((NF, W, 3 * Kc), BF16)
-
-    @pl.when(attends)
-    def _():
-        drain(dall.at[pl.ds(0, NF - 1)], dsem.at[1])
-
-    @pl.when(jnp.logical_not(attends))
-    def _():
-        drain(dall.at[pl.ds(0, (C - 1) * T)], dsem.at[1])
-
-    activate(1)
-
-    def neighbour(row, edge, outermost):
-        @pl.when(edge)
-        def _():
-            drain(dall.at[pl.ds(0, NF - 1)], dsem.at[row])
-
-        @pl.when(outermost)
-        def _():
-            drain(dall.at[pl.ds(0, (C - 1) * T)], dsem.at[row])
-
-        @pl.when(jnp.logical_not(edge | outermost))
-        def _():
-            drain(dall.at[pl.ds(0, NF)], dsem.at[row])
-
-        activate(row)
-
-    pl.when(h > 0)(lambda: neighbour(0, h == 1, h == S - 1))
-    pl.when(h < S - 1)(lambda: neighbour(2, h == S - 2, h == 0))
 
     if not skips:
         pl.when(h == 0)(lambda: blank(0))
         pl.when(h == S - 1)(lambda: blank(2))
 
-    loads[4].wait()
+    def row_in(row, k, own, outermost):
+        lacks_one = outermost | (own & (t == k))
+
+        @pl.when(lacks_one)
+        def _():
+            drain(dall.at[pl.ds(0, C - 1)], dsem.at[row, k])
+
+        @pl.when(jnp.logical_not(lacks_one))
+        def _():
+            drain(dall.at[pl.ds(0, C)], dsem.at[row, k])
+
+        activate(row, k)
+
+    def block_in(k):
+        if k:
+            pl.when(jnp.logical_not(attends) & (t >= k))(lambda: forward(k))
+        row_in(1, k, attends, jnp.logical_not(attends))
+        pl.when(h > 0)(lambda: row_in(0, k, h == 1, h == S - 1))
+        pl.when(h < S - 1)(lambda: row_in(2, k, h == S - 2, h == 0))
+
     wide = half // CHUNKS
 
-    def product(to, a0, b0, b1, chunk):
+    def product(to, b0, b1, chunk):
         total = None
         taps = slice(b0 * 3 * Kc, b1 * 3 * Kc)
-        for a in range(a0, 3):
-            window = act[pl.ds(to * C + a, C), :, taps].reshape(C * W, (b1 - b0) * 3 * Kc)
+        for a in range(0 if to else max(0, 3 - C), 3):
+            window = act[to * C + a : to * C + a + C, :, taps].reshape(C * W, (b1 - b0) * 3 * Kc)
             weight = wc[a, taps, chunk * wide : (chunk + 1) * wide]
             term = jnp.dot(window, weight, preferred_element_type=F32)
             total = term if total is None else total + term
@@ -406,31 +401,29 @@
     else:
         edges = [(h == 0, 1, 3), (h == S - 1, 0, 2), (attends, 0, 3)]
 
-    def partial(to, store):
+    def store(to, chunk, value):
+        @pl.when(t == to)
+        def _():
+            own_total[chunk] = value
+
+        @pl.when(t != to)
+        def _():
+            away = lax.rem(to - t + T, T) - 1
+            part_src[away, chunk] = value.astype(BF16)
+            send(part_src.at[away, chunk], part.at[away, chunk], psend, psem.at[away, chunk], (g, h, to, c))
+
+    for k in range(T):
+        block_in(k)
+        if not k:
+            loads[4].wait()
         for here, b0, b1 in edges:
-            for early, a0 in ((to == 0, max(0, 3 - C)), (to > 0, 0)):
-
-                @pl.when(here & early)
-                def _():
-                    for chunk in range(CHUNKS):
-                        store(chunk, product(to, a0, b0, b1, chunk))
-
-    for dt in range(1, T):
-
-        def send_part(chunk, value):
-            part_src[dt - 1, chunk] = value.astype(BF16)
-            send(
-                part_src.at[dt - 1, chunk], part.at[dt - 1, chunk], psend, psem.at[dt - 1, chunk],
-                (g, h, lax.rem(t + dt, T), c),
-            )
-
-        partial(lax.rem(t + dt, T), send_part)
-
-
-    def keep(chunk, value):
-        own_total[chunk] = value
-
-    partial(t, keep)
+
+            @pl.when(here)
+            def _():
+                for chunk in range(CHUNKS):
+                    store(k, chunk, product(k, b0, b1, chunk))
+
+
     @pl.when(attends)
     def _():
         drain(att_in.at[pl.ds(0, C - 1)], asem)
@@ -539,7 +532,7 @@
             dma(()),
             dma(()),
             dma((2,)),
-            dma((3,)),
+            dma((3, T)),
             dma((2, T)),
             dma(()),
             dma(()),

time: 23 us -> 22.6 us (0.983)
  Pallas kernels: 22.2 us -> 21.8 us
    pallas_call x1, Pallas kernels: 21.6 us -> 21.1 us  [on_device(): pl.pallas_call(functools.partial(kernel, S, T, C, W), out_shape=(kept, ke...]
where the time goes in v4:
time: 22.6 us; the launch traced here: 22.4 us
  Pallas kernels  21.8 us (96%)
  between operations  0.64 us (3%)
    pallas_call x1, Pallas kernels, on_device(): pl.pallas_call(functools.partial(kernel, S, T, C, W), out_shape=(kept, ke...  21.1 us
    pallas_call x1, Pallas kernels, on_device(): pl.pallas_call(hand_over, out_shape=(out, out), in_specs=[vmem] * 2, out_...  0.66 us

profile of v4, /device:TPU:0, one launch (start us, length us, event | category | flops | bytes accessed | tf_op | source)
XLA Modules:
  0.0 22.4 jit_solution(17764566468932795901)
XLA Ops:
  0.6 21.1 %shard_map.95 = (bf16[2,1,64,256]{3,2,1,0:T(8,128)(2,1)S(1)}, bf16[2,1,64,256]{3,2,1,0:T(8,128)(2,1)S(1)}) custom-call(bf16[2,1,64,256]{3,2,1,0:T(8,128)(2,1)} %x_hbm.1, f32[1,256]{1,0:T(1,128)} %bitcast.4, f32[1,256]{1,0:T(1,128)} %bitcast.5, bf16[512,512]{1,0:T(8,128)(2,1)} %wq_hbm.1, bf16[512,512]{1,0:T(8,128)(2,1)} %wk_hbm.1, bf16[512,512]{1,0:T(8,128)(2,1)} %wv_hbm.1, ...), custom_call_target="tpu_custom_call" | custom-call | tf_op jit(solution)/shard_map/pallas_call | solution.py:494
  21.8 0.7 %shard_map.96 = (bf16[2,1,64,256]{3,2,1,0:T(8,128)(2,1)}, bf16[2,1,64,256]{3,2,1,0:T(8,128)(2,1)}) custom-call(bf16[2,1,64,256]{3,2,1,0:T(8,128)(2,1)S(1)} %get-tuple-element.4.att_in, bf16[2,1,64,256]{3,2,1,0:T(8,128)(2,1)S(1)} %get-tuple-element.5.conv_in), custom_call_target="tpu_custom_call" | custom-call | tf_op jit(solution)/shard_map/pallas_call | solution.py:543

commit v5 on v4

--- a/solution.py
+++ b/solution.py
@@ -23,26 +23,38 @@
     width = v.shape[1]
     step = 1
     while step < GROUP:
-        above = pltpu.roll(v, width - step, 1)
-        below = pltpu.roll(v, step, 1)
-        v = v + jnp.where((lane // step) % 2 == 0, above, below)
-        step *= 2
+        place = (lane // step) % 4
+        terms = [v]
+        for d in range(1, 4):
+            terms.append(jnp.where(place < 4 - d, pltpu.roll(v, width - d * step, 1), 0.0))
+            terms.append(jnp.where(place >= d, pltpu.roll(v, d * step, 1), 0.0))
+        while len(terms) > 1:
+            terms = [sum(terms[i : i + 2]) for i in range(0, len(terms), 2)]
+        v = terms[0]
+        step *= 4
     return v
 
 
-def channel_sums(values):
-    return jnp.sum(values, axis=0, keepdims=True), jnp.sum(values * values, axis=0, keepdims=True)
-
-
-def moments(totals, population):
-    blocks = totals.shape[1] // LANES
-    pieces = [totals[k : k + 1, b * LANES : (b + 1) * LANES] for k in range(2) for b in range(blocks)]
-    rows = 8 * pl.cdiv(2 * blocks, 8)
-    grouped = group_total(jnp.concatenate(pieces + pieces[:1] * (rows - 2 * blocks), axis=0)) / population
-    mean = jnp.concatenate([grouped[b : b + 1] for b in range(blocks)], axis=1)
-    square = jnp.concatenate([grouped[blocks + b : blocks + b + 1] for b in range(blocks)], axis=1)
-    variance = jnp.maximum(square - mean * mean, 0.0)
-    return mean, lax.rsqrt(variance + EPSILON)
+def store_sums(ref, values):
+    sums = jnp.sum(values, axis=0, keepdims=True)
+    squares = jnp.sum(values * values, axis=0, keepdims=True)
+    blocks, width = ref.shape[0] // 2, ref.shape[1]
+    for b in range(blocks):
+        ref[b : b + 1] = sums[:, b * width : (b + 1) * width]
+        ref[blocks + b : blocks + b + 1] = squares[:, b * width : (b + 1) * width]
+
+
+def moments(stacks, population):
+    size = stacks[0].shape[0]
+    blocks = size // 2
+    count = len(stacks) * size
+    rows = 8 * pl.cdiv(count, 8)
+    padding = [jnp.zeros((rows - count, LANES), F32)] if rows > count else []
+    grouped = group_total(jnp.concatenate([*stacks, *padding], axis=0)) / population
+    variance = jnp.maximum(pltpu.roll(grouped, rows - blocks, 0) - grouped * grouped, 0.0)
+    scale = lax.rsqrt(variance + EPSILON)
+    picks = [i * size + b for i in range(len(stacks)) for b in range(blocks)]
+    return [jnp.concatenate([v[k : k + 1] for k in picks], axis=1) for v in (grouped, scale)]
 
 
 def kernel(
@@ -50,9 +62,9 @@
     x_hbm, g1, g2, wq_hbm, wk_hbm, wv_hbm, wo_hbm, wc_hbm,
     att_out, conv_out,
     x, projections, wo, wc,
-    stat1_src, stat1, stat2_src, stat2, gall,
+    stat1_src, row_sum, stat1, stat2_src, stat2, gall,
     xall, tokens, keyed, valued, att_src, att_in, dsrc, dall, act, own_total, part_src, part,
-    xload, wsem, insem, gsend, gsem, s1send, s1sem, xsend, xsem, s2send, s2sem,
+    xload, wsem, insem, gsend, gsem, raw_sem, s1send, s1sem, xsend, xsem, s2send, s2sem,
     asend, asem, dsend, dsem, outer_sem, share_sem, psend, psem,
 ):
     g = lax.axis_index("groups")
@@ -82,13 +94,16 @@
             for dc in range(C):
                 act_on((g, r, lax.rem(t + dt, T), lax.rem(c + dc, C)))
 
-    def beside(sign, act_on):
+    def row_where(r, sign, act_on):
         for dt in range(1, T):
 
             @pl.when((t + sign * dt >= 0) & (t + sign * dt < T))
             def _():
                 for dc in range(C):
-                    act_on((g, h, t + sign * dt, lax.rem(c + dc, C)))
+                    act_on((g, r, t + sign * dt, lax.rem(c + dc, C)))
+
+    def beside(sign, act_on):
+        row_where(h, sign, act_on)
 
     def mates(act_on):
         for dc in range(1, C):
@@ -111,21 +126,23 @@
     x_load.start()
     for k, gain in enumerate((g1, g2)):
         pltpu.make_async_copy(gain, gall.at[c, k], xload.at[1]).start()
+    stat1[...] = jnp.zeros(stat1.shape, F32)
     barrier = pltpu.get_barrier_semaphore()
     mates(signal(barrier))
-    pl.when(attends)(lambda: beside(-1, signal(barrier)))
-    rows_apart(1, lambda r, d: row_devices(r, signal(barrier)))
-    pl.semaphore_wait(barrier, (h * T + jnp.where(attends, T - 1 - t, 0)) * C + C - 1)
-
-    def answer(r, d):
-        for dt in range(T):
-            for dc in range(C):
-                signal(insem.at[min(dt, 1), d])((g, r, lax.rem(t + dt, T), lax.rem(c + dc, C)))
-
-    @pl.when(h < S - 1)
-    def _():
-        rows_apart(-1, answer)
-        pl.when(h > 0)(lambda: beside(1, signal(insem.at[0, 0])))
+    beside(1, signal(barrier))
+
+    def column(r, act_on):
+        for dc in range(C):
+            act_on((g, r, t, lax.rem(c + dc, C)))
+
+    def greet(r, d):
+        column(r, signal(barrier))
+        row_where(r, 1, signal(barrier))
+
+    rows_apart(1, greet)
+    pl.semaphore_wait(barrier, (h * (t + 1) + t) * C + C - 1)
+    pl.when(h < S - 1)(lambda: rows_apart(-1, lambda r, d: column(r, signal(insem.at[d]))))
+    beside(-1, signal(insem.at[0]))
 
     loads = [
         pltpu.make_async_copy(src, dst, wsem.at[i])
@@ -140,13 +157,23 @@
     loads[4].start()
 
     x_load.wait()
-    sums, squares = channel_sums(x[...].reshape(C * W, half).astype(F32))
-    stat1_src[0:1] = sums
-    stat1_src[1:2] = squares
+    store_sums(stat1_src, x[...].reshape(C * W, half).astype(F32))
     at = (h * T + t) * C + c
 
-    def send_stat(where):
-        send(stat1_src, stat1.at[at], s1send, s1sem, where)
+    def send_stat(where, src=stat1_src, recvs=s1sem):
+        send(src, stat1.at[at], s1send, recvs, where)
+
+    def same_row(sign):
+        for dt in range(1, T):
+
+            @pl.when((t + sign * dt >= 0) & (t + sign * dt < T))
+            def _():
+                send_stat((g, h, t + sign * dt, c), recvs=raw_sem)
+
+                @pl.when(attends)
+                def _():
+                    for dc in range(1, C):
+                        send_stat((g, h, t + sign * dt, lax.rem(c + dc, C)))
 
     def send_x(r, dc):
         frame = lax.rem(c + dc, C)
@@ -157,12 +184,17 @@
             send_x(r, dc)
 
     for r in range(1, S - 1):
-        pl.when(r < h)(lambda: row_devices(r, send_stat))
+
+        @pl.when(r < h)
+        def _():
+            column(r, send_stat)
+            row_where(r, -1, send_stat)
+
+    pl.when(h < S - 1)(lambda: same_row(-1))
+    stat1[at] = stat1_src[...]
 
     @pl.when(attends)
     def _():
-        stat1[at] = stat1_src[...]
-        beside(1, send_stat)
         mates(send_stat)
         xall[h * C + c] = x[c, 0]
         for dc in range(1, C):
@@ -174,25 +206,43 @@
     drain(gall.at[c], xload.at[1])
     mates(lambda where: send(gall.at[c], gall.at[c], gsend, gsem, where))
 
-    def upward(r, d):
-        @pl.when(r < S - 1)
-        def _():
-            pl.semaphore_wait(insem.at[0, d], C)
-            for dc in range(C):
-                send_stat((g, r, t, lax.rem(c + dc, C)))
-            column_x(r)
-            if T > 1:
-                pl.semaphore_wait(insem.at[1, d], (T - 1) * C)
-            for dt in range(1, T):
-                for dc in range(C):
-                    send_stat((g, r, lax.rem(t + dt, T), lax.rem(c + dc, C)))
-
-    rows_apart(1, upward)
-
-    @pl.when(attends & (t > 0))
-    def _():
-        pl.semaphore_wait(insem.at[0, 0], t * C)
-        beside(-1, send_stat)
+    @pl.when(h < S - 2)
+    def _():
+        pl.semaphore_wait(insem.at[1], C)
+        column_x(h + 1)
+
+    @pl.when(t < T - 1)
+    def _():
+        pl.semaphore_wait(insem.at[0], (T - 1 - t) * C)
+        for r in range(1, S - 1):
+            pl.when(r < h)(lambda: row_where(r, 1, send_stat))
+        pl.when(h < S - 1)(lambda: same_row(1))
+
+    @pl.when(h < S - 1)
+    def _():
+        if T > 1:
+            drain(stat1.at[pl.ds(0, T - 1)], raw_sem)
+
+    @pl.when(h < S - 2)
+    def _():
+        total = stat1_src[...]
+        for dt in range(1, T):
+            total = total + stat1[(h * T + lax.rem(t + dt, T)) * C + c]
+        row_sum[...] = total
+
+        def send_sum(where):
+            send_stat(where, src=row_sum)
+
+        column(h + 1, send_sum)
+
+        def upward(d):
+            @pl.when(h + d < S - 1)
+            def _():
+                pl.semaphore_wait(insem.at[d], C)
+                column(h + d, send_sum)
+                column_x(h + d)
+
+        pl.loop(2, S - 1, unroll=S <= 4)(upward)
 
     drain(gall.at[pl.ds(0, C - 1)], gsem)
     population = float(S * T * C * W * GROUP)
@@ -209,9 +259,24 @@
         def rest(i):
             return i + skipped if R == 2 else i + jnp.where(i >= h, 1, 0)
 
-        drain(stat1.at[pl.ds(0, S * T * C - 1)], s1sem)
-        totals = jnp.sum(stat1[...].reshape(S * T, C, 2, half), axis=0)
-        mean1, scale1 = moments(jnp.concatenate([totals[k] for k in range(C)], axis=1), population)
+        def slots_in(r):
+            drain(xall.at[pl.ds(r * C, C)], xsem.at[r])
+
+        for r in range(1, S - 1):
+
+            @pl.when(h == r)
+            def _():
+                drain(stat1.at[pl.ds(0, r * C + T * (C - 1) + (S - 1 - r) * T * C)], s1sem)
+
+        drain(xall.at[pl.ds(0, C - 1)], xsem.at[h])
+        if R == 2:
+            slots_in(outer)
+        for i in range(S - R):
+            slots_in(rest(i))
+        drain(projections, wsem.at[0])
+        drain(wo, wsem.at[1])
+        totals = jnp.sum(stat1[...].reshape(S * T, C, *stat1.shape[1:]), axis=0)
+        mean1, scale1 = moments([totals[k] for k in range(C)], population)
         factor1 = scale1 * jnp.concatenate([gall[k, 0] for k in range(C)], axis=1)
 
         def row_tokens(r):
@@ -226,20 +291,11 @@
             rows = tokens[first:stop].reshape((stop - first) * W, D)
             return jnp.dot(rows, weight[...], preferred_element_type=F32).astype(BF16)
 
-        def slots_in(r):
-            drain(xall.at[pl.ds(r * C, C)], xsem.at[r])
-
-        drain(xall.at[pl.ds(0, C - 1)], xsem.at[h])
-        if R == 2:
-            slots_in(outer)
         for i in range(R):
             tokens[i] = row_tokens(mine[i])
-        drain(projections, wsem.at[0])
-        queries = project(projections.at[0], 0, R)
-        for i in range(S - R):
-            slots_in(rest(i))
         for i in range(S - R):
             tokens[R + i] = row_tokens(rest(i))
+        queries = project(projections.at[0], 0, R)
         keyed[...] = project(projections.at[1], 0, S)
         valued[...] = project(projections.at[2], 0, S)
 
@@ -249,8 +305,7 @@
         weights = jnp.exp(scores - jnp.max(scores, axis=1, keepdims=True))
         mass = jnp.sum(weights, axis=1, keepdims=True)
         mixed = jnp.dot(weights.astype(BF16), valued[...], preferred_element_type=F32)
-        mixed = (mixed / mass).astype(BF16)
-        loads[3].wait()
+        mixed = (mixed * (1.0 / mass)).astype(BF16)
         attended = jnp.dot(mixed, wo[...], preferred_element_type=F32).astype(BF16)
 
         source = jnp.concatenate(
@@ -275,11 +330,8 @@
             for own in (False, True):
                 for i in range(2):
                     send_row(i, outer, [0], dsend.at[0], outer_sem.at[i, t], own=own)
-        sums, squares = channel_sums(resid)
         for k in range(T):
-            lanes = slice(k * Kc, (k + 1) * Kc)
-            stat2_src[k, 0:1] = sums[:, lanes]
-            stat2_src[k, 1:2] = squares[:, lanes]
+            store_sums(stat2_src.at[k], resid[:, k * Kc : (k + 1) * Kc])
 
         def send_stat2(where):
             send(stat2_src.at[where[2]], stat2.at[me], s2send, s2sem, where)
@@ -428,7 +480,6 @@
     def _():
         drain(att_in.at[pl.ds(0, C - 1)], asem)
         att_out[other, 0] = att_in[other]
-        drain(stat1.at[pl.ds(0, attending - 1)], s1send)
         drain(xall.at[pl.ds(0, (S - 2) * C - 1)], xsend)
         drain(stat2.at[pl.ds(0, S * T * C - 1)], s2send)
 
@@ -437,9 +488,17 @@
         drain(att_in, asem)
         for k in range(C):
             att_out[k, 0] = att_in[k]
-        drain(stat1.at[pl.ds(0, attending)], s1send)
         drain(xall.at[pl.ds(0, (S - 2) * C)], xsend)
         drain(dall.at[pl.ds(0, 2 * T * (C - 1))], share_sem)
+
+    for r in range(S):
+
+        @pl.when(h == r)
+        def _():
+            below = max(r - 1, 0) if r < S - 1 else S - 2
+            level = (T - 1 if r == 0 else T * C - 1) if r < S - 1 else 0
+            above = max(S - 2 - r, 0)
+            drain(stat1.at[pl.ds(0, below * T * C + level + above * C)], s1send)
 
     @pl.when(attends & jnp.logical_not(at_edge))
     def _():
@@ -464,12 +523,11 @@
 
 
 def slice_moments(totals, population):
-    Kc = totals.shape[1]
-    if Kc >= LANES:
-        return moments(totals, population)
-    padded = jnp.concatenate([totals] * (LANES // Kc), axis=1)
-    mean, scale = moments(padded, population)
-    return mean[:, :Kc], scale[:, :Kc]
+    width = totals.shape[1]
+    if width == LANES:
+        return moments([totals], population)
+    mean, scale = moments([jnp.concatenate([totals] * (LANES // width), axis=1)], population)
+    return mean[:, :width], scale[:, :width]
 
 
 def hand_over(att_in, conv_in, att_out, conv_out):
@@ -491,6 +549,7 @@
     dma = pltpu.SemaphoreType.DMA
     kept = pltpu.VMEM(x.shape, BF16)
     links = max(T - 1, 1)
+    stats = (2 * max(Kc // LANES, 1), min(Kc, LANES))
     results = pl.pallas_call(
         functools.partial(kernel, S, T, C, W),
         out_shape=(kept, kept),
@@ -501,10 +560,11 @@
             pltpu.VMEM((3, D, D), BF16),
             pltpu.VMEM((D, D), BF16),
             pltpu.VMEM(wc.shape, BF16),
-            pltpu.VMEM((2, half), F32),
-            pltpu.VMEM((n, 2, half), F32),
-            pltpu.VMEM((T, 2, Kc), F32),
-            pltpu.VMEM((n, 2, Kc), F32),
+            pltpu.VMEM((half // 64, LANES), F32),
+            pltpu.VMEM((half // 64, LANES), F32),
+            pltpu.VMEM((n, half // 64, LANES), F32),
+            pltpu.VMEM((T, *stats), F32),
+            pltpu.VMEM((n, *stats), F32),
             pltpu.VMEM((C, 2, 1, half), F32),
             pltpu.VMEM((S * C, W, half), BF16),
             pltpu.VMEM((S, W, D), BF16),
@@ -520,7 +580,8 @@
             pltpu.VMEM((links, CHUNKS, C * W, wide), BF16),
             dma((2,)),
             dma((3,)),
-            pltpu.SemaphoreType.REGULAR((2, S - 1)),
+            pltpu.SemaphoreType.REGULAR((S - 1,)),
+            dma(()),
             dma(()),
             dma(()),
             dma(()),

time: 22.6 us -> 22.5 us (level)
  no operation moved by 1% of the time
where the time goes in v5:
time: 22.5 us; the launch traced here: 22.4 us
  Pallas kernels  21.7 us (96%)
  between operations  0.64 us (3%)
    pallas_call x1, Pallas kernels, on_device(): pl.pallas_call(functools.partial(kernel, S, T, C, W), out_shape=(kept, ke...  21.1 us
    pallas_call x1, Pallas kernels, on_device(): pl.pallas_call(hand_over, out_shape=(out, out), in_specs=[vmem] * 2, out_...  0.66 us

profile of v5, /device:TPU:0, one launch (start us, length us, event | category | flops | bytes accessed | tf_op | source)
XLA Modules:
  0.0 22.4 jit_solution(13881302274626755301)
XLA Ops:
  0.6 21.1 %shard_map.95 = (bf16[2,1,64,256]{3,2,1,0:T(8,128)(2,1)S(1)}, bf16[2,1,64,256]{3,2,1,0:T(8,128)(2,1)S(1)}) custom-call(bf16[2,1,64,256]{3,2,1,0:T(8,128)(2,1)} %x_hbm.1, f32[1,256]{1,0:T(1,128)} %bitcast.4, f32[1,256]{1,0:T(1,128)} %bitcast.5, bf16[512,512]{1,0:T(8,128)(2,1)} %wq_hbm.1, bf16[512,512]{1,0:T(8,128)(2,1)} %wk_hbm.1, bf16[512,512]{1,0:T(8,128)(2,1)} %wv_hbm.1, ...), custom_call_target="tpu_custom_call" | custom-call | tf_op jit(solution)/shard_map/pallas_call | solution.py:553
  21.7 0.7 %shard_map.96 = (bf16[2,1,64,256]{3,2,1,0:T(8,128)(2,1)}, bf16[2,1,64,256]{3,2,1,0:T(8,128)(2,1)}) custom-call(bf16[2,1,64,256]{3,2,1,0:T(8,128)(2,1)S(1)} %get-tuple-element.4.att_in, bf16[2,1,64,256]{3,2,1,0:T(8,128)(2,1)S(1)} %get-tuple-element.5.conv_in), custom_call_target="tpu_custom_call" | custom-call | tf_op jit(solution)/shard_map/pallas_call | solution.py:604

commit v6 on v5

--- a/solution.py
+++ b/solution.py
@@ -326,10 +326,6 @@
                             (g, r, to, lax.rem(c + dc, C)),
                         )
 
-        if R == 2:
-            for own in (False, True):
-                for i in range(2):
-                    send_row(i, outer, [0], dsend.at[0], outer_sem.at[i, t], own=own)
         for k in range(T):
             store_sums(stat2_src.at[k], resid[:, k * Kc : (k + 1) * Kc])
 
@@ -341,6 +337,10 @@
         beside(-1, send_stat2)
         beside(1, send_stat2)
         mates(send_stat2)
+        if R == 2:
+            for own in (False, True):
+                for i in range(2):
+                    send_row(i, outer, [0], dsend.at[0], outer_sem.at[i, t], own=own)
         if R == 2:
             send_row(0, h - side, everyone, dsend.at[1], dsem.at[1 + side, t])
         else:

time: 22.5 us -> 21.3 us (0.947)
  Pallas kernels: 21.7 us -> 20.5 us
    pallas_call x1, Pallas kernels: 21.1 us -> 19.9 us  [on_device(): pl.pallas_call(functools.partial(kernel, S, T, C, W), out_shape=(kept, ke...]
where the time goes in v6:
time: 21.3 us; the launch traced here: 21.2 us
  Pallas kernels  20.5 us (96%)
  between operations  0.64 us (3%)
    pallas_call x1, Pallas kernels, on_device(): pl.pallas_call(functools.partial(kernel, S, T, C, W), out_shape=(kept, ke...  19.9 us
    pallas_call x1, Pallas kernels, on_device(): pl.pallas_call(hand_over, out_shape=(out, out), in_specs=[vmem] * 2, out_...  0.66 us

profile of v6, /device:TPU:0, one launch (start us, length us, event | category | flops | bytes accessed | tf_op | source)
XLA Modules:
  0.0 21.2 jit_solution(1504394259901755288)
XLA Ops:
  0.6 19.9 %shard_map.95 = (bf16[2,1,64,256]{3,2,1,0:T(8,128)(2,1)S(1)}, bf16[2,1,64,256]{3,2,1,0:T(8,128)(2,1)S(1)}) custom-call(bf16[2,1,64,256]{3,2,1,0:T(8,128)(2,1)} %x_hbm.1, f32[1,256]{1,0:T(1,128)} %bitcast.4, f32[1,256]{1,0:T(1,128)} %bitcast.5, bf16[512,512]{1,0:T(8,128)(2,1)} %wq_hbm.1, bf16[512,512]{1,0:T(8,128)(2,1)} %wk_hbm.1, bf16[512,512]{1,0:T(8,128)(2,1)} %wv_hbm.1, ...), custom_call_target="tpu_custom_call" | custom-call | tf_op jit(solution)/shard_map/pallas_call | solution.py:553
  20.5 0.7 %shard_map.96 = (bf16[2,1,64,256]{3,2,1,0:T(8,128)(2,1)}, bf16[2,1,64,256]{3,2,1,0:T(8,128)(2,1)}) custom-call(bf16[2,1,64,256]{3,2,1,0:T(8,128)(2,1)S(1)} %get-tuple-element.4.att_in, bf16[2,1,64,256]{3,2,1,0:T(8,128)(2,1)S(1)} %get-tuple-element.5.conv_in), custom_call_target="tpu_custom_call" | custom-call | tf_op jit(solution)/shard_map/pallas_call | solution.py:604

commit v7 on v6

--- a/solution.py
+++ b/solution.py
@@ -453,28 +453,33 @@
     else:
         edges = [(h == 0, 1, 3), (h == S - 1, 0, 2), (attends, 0, 3)]
 
-    def store(to, chunk, value):
-        @pl.when(t == to)
-        def _():
-            own_total[chunk] = value
-
-        @pl.when(t != to)
-        def _():
-            away = lax.rem(to - t + T, T) - 1
-            part_src[away, chunk] = value.astype(BF16)
-            send(part_src.at[away, chunk], part.at[away, chunk], psend, psem.at[away, chunk], (g, h, to, c))
-
-    for k in range(T):
-        block_in(k)
-        if not k:
-            loads[4].wait()
+    def convolve(to, store):
         for here, b0, b1 in edges:
 
             @pl.when(here)
             def _():
                 for chunk in range(CHUNKS):
-                    store(k, chunk, product(k, b0, b1, chunk))
-
+                    store(chunk, product(to, b0, b1, chunk))
+
+    def convolve_away(to):
+        away = lax.rem(to - t + T, T) - 1
+
+        def store(chunk, value):
+            part_src[away, chunk] = value.astype(BF16)
+            send(part_src.at[away, chunk], part.at[away, chunk], psend, psem.at[away, chunk], (g, h, to, c))
+
+        convolve(to, store)
+
+    def keep(chunk, value):
+        own_total[chunk] = value
+
+    loads[4].wait()
+    for k in range(T):
+        block_in(k)
+        pl.when(t != k)(lambda: convolve_away(k))
+
+    for k in range(T):
+        pl.when(t == k)(lambda: convolve(k, keep))
 
     @pl.when(attends)
     def _():

time: 21.3 us -> 20.8 us (0.977)
  Pallas kernels: 20.5 us -> 19.9 us
    pallas_call x1, Pallas kernels: 19.9 us -> 19.2 us  [on_device(): pl.pallas_call(functools.partial(kernel, S, T, C, W), out_shape=(kept, ke...]
where the time goes in v7:
time: 20.8 us; the launch traced here: 20.5 us
  Pallas kernels  19.9 us (96%)
  between operations  0.64 us (3%)
    pallas_call x1, Pallas kernels, on_device(): pl.pallas_call(functools.partial(kernel, S, T, C, W), out_shape=(kept, ke...  19.2 us
    pallas_call x1, Pallas kernels, on_device(): pl.pallas_call(hand_over, out_shape=(out, out), in_specs=[vmem] * 2, out_...  0.66 us

profile of v7, /device:TPU:0, one launch (start us, length us, event | category | flops | bytes accessed | tf_op | source)
XLA Modules:
  0.0 20.5 jit_solution(15349956200418834893)
XLA Ops:
  0.6 19.2 %shard_map.95 = (bf16[2,1,64,256]{3,2,1,0:T(8,128)(2,1)S(1)}, bf16[2,1,64,256]{3,2,1,0:T(8,128)(2,1)S(1)}) custom-call(bf16[2,1,64,256]{3,2,1,0:T(8,128)(2,1)} %x_hbm.1, f32[1,256]{1,0:T(1,128)} %bitcast.4, f32[1,256]{1,0:T(1,128)} %bitcast.5, bf16[512,512]{1,0:T(8,128)(2,1)} %wq_hbm.1, bf16[512,512]{1,0:T(8,128)(2,1)} %wk_hbm.1, bf16[512,512]{1,0:T(8,128)(2,1)} %wv_hbm.1, ...), custom_call_target="tpu_custom_call" | custom-call | tf_op jit(solution)/shard_map/pallas_call | solution.py:558
  19.9 0.7 %shard_map.96 = (bf16[2,1,64,256]{3,2,1,0:T(8,128)(2,1)}, bf16[2,1,64,256]{3,2,1,0:T(8,128)(2,1)}) custom-call(bf16[2,1,64,256]{3,2,1,0:T(8,128)(2,1)S(1)} %get-tuple-element.4.att_in, bf16[2,1,64,256]{3,2,1,0:T(8,128)(2,1)S(1)} %get-tuple-element.5.conv_in), custom_call_target="tpu_custom_call" | custom-call | tf_op jit(solution)/shard_map/pallas_call | solution.py:609

commit v8 on v7

--- a/solution.py
+++ b/solution.py
@@ -65,7 +65,7 @@
     stat1_src, row_sum, stat1, stat2_src, stat2, gall,
     xall, tokens, keyed, valued, att_src, att_in, dsrc, dall, act, own_total, part_src, part,
     xload, wsem, insem, gsend, gsem, raw_sem, s1send, s1sem, xsend, xsem, s2send, s2sem,
-    asend, asem, dsend, dsem, outer_sem, share_sem, psend, psem,
+    asend, asem, dsend, dsem, direct_sem, share_sem, psend, psem,
 ):
     g = lax.axis_index("groups")
     h = lax.axis_index("space")
@@ -121,7 +121,6 @@
         )
         copy.start()
 
-    everyone = range(C)
     x_load = pltpu.make_async_copy(x_hbm, x, xload.at[0])
     x_load.start()
     for k, gain in enumerate((g1, g2)):
@@ -316,16 +315,15 @@
             for k in range(T):
                 dsrc[i, k] = resid[i * W : (i + 1) * W, k * Kc : (k + 1) * Kc].astype(BF16)
 
-        def send_row(i, r, cores, sends, recv, skip_self=False, own=None):
-            for dt in {None: [*range(1, T), 0], False: range(1, T), True: [0]}[own]:
-                for dc in cores:
-                    if not (skip_self and dt == 0 and dc == 0):
-                        to = lax.rem(t + dt, T)
-                        send(
-                            dsrc.at[i, to], dall.at[(mine[i] - r + 1) * NF + frame_at], sends, recv,
-                            (g, r, to, lax.rem(c + dc, C)),
-                        )
-
+        def send_row(i, r, columns, sends):
+            for dt in columns:
+                to = lax.rem(t + dt, T)
+                row = mine[i] - r + 1
+                send(
+                    dsrc.at[i, to], dall.at[row * NF + frame_at], sends, direct_sem.at[row, t], (g, r, to, c),
+                )
+
+        others = range(1, T)
         for k in range(T):
             store_sums(stat2_src.at[k], resid[:, k * Kc : (k + 1) * Kc])
 
@@ -338,27 +336,27 @@
         beside(1, send_stat2)
         mates(send_stat2)
         if R == 2:
-            for own in (False, True):
-                for i in range(2):
-                    send_row(i, outer, [0], dsend.at[0], outer_sem.at[i, t], own=own)
-        if R == 2:
-            send_row(0, h - side, everyone, dsend.at[1], dsem.at[1 + side, t])
+            for i in range(2):
+                send_row(i, outer, others, dsend.at[0])
+            send_row(0, h - side, [*others, 0], dsend.at[1])
         else:
-            send_row(0, h - 1, everyone, dsend.at[1], dsem.at[2, t])
-            send_row(0, h + 1, everyone, dsend.at[1], dsem.at[0, t])
+            for r in (h - 1, h + 1):
+                send_row(0, r, [*others, 0], dsend.at[1])
         for i in range(R):
-            row = mine[i] - h + 1
-            send_row(i, h, everyone, dsend.at[1], dsem.at[row, t], skip_self=True)
-            dall[row * NF + frame_at] = dsrc[i, t]
+            send_row(i, h, others, dsend.at[1])
+            slot = (mine[i] - h + 1) * NF + frame_at
+            mates(lambda where: send(dsrc.at[i, t], dall.at[slot], dsend.at[1], dsem.at[mine[i] - h + 1, t], where))
+            dall[slot] = dsrc[i, t]
         for i in range(R):
             for k in range(C):
                 att_src[i, k] = attended[i * W : (i + 1) * W, k * half : (k + 1) * half]
-        send_attended(0, other, h, other)
-        if R == 2:
-            for k in range(C):
-                send_attended(1, k, outer, k)
         stat2[me] = stat2_src[t]
         att_out[c, 0] = att_src[0, c]
+        if R == 2:
+            if T > 1:
+                drain(dall.at[pl.ds(0, 2 * (T - 1))], dsend.at[0])
+            for i in range(2):
+                send_row(i, outer, [0], dsend.at[2])
 
     if S > 4:
         pl.when(attends & jnp.logical_not(at_edge))(lambda: attend(1))
@@ -366,25 +364,35 @@
     act[0:2] = jnp.zeros((2,) + act.shape[1:], BF16)
     gain2 = jnp.concatenate([gall[k, 1] for k in range(C)], axis=1)
 
-    beyond = jnp.where(h == 0, 1, 0)
+    rows = [(0, h > 0, h == 1), (1, h >= 0, attends), (2, h < S - 1, h == S - 2)]
 
     def forward(k):
-        for i in range(2):
-            row = beyond + i
-            slot = row * NF + k * C + c
-            drain(dall.at[slot], outer_sem.at[jnp.where(h == 0, 1 - i, i), k])
-            mates(lambda where: send(dall.at[slot], dall.at[slot], share_sem, dsem.at[row, k], where))
+        for row, there, made_here in rows:
+
+            @pl.when(there & jnp.logical_not(made_here & (t == k)))
+            def _():
+                slot = row * NF + k * C + c
+                drain(dall.at[slot], direct_sem.at[row, k])
+                mates(lambda where: send(dall.at[slot], dall.at[slot], share_sem, dsem.at[row, k], where))
+
+
+    forward(0)
+    for k in range(1, T):
+        pl.when(t < k)(lambda: forward(k))
 
     @pl.when(jnp.logical_not(attends))
     def _():
-        forward(0)
-        for k in range(1, T):
-            pl.when(t < k)(lambda: forward(k))
         drain(stat2.at[pl.ds(0, attending)], s2sem)
 
     @pl.when(attends)
     def _():
         drain(stat2.at[pl.ds(0, attending - 1)], s2sem)
+        send_attended(0, other, h, other)
+
+    @pl.when(at_edge)
+    def _():
+        for k in range(C):
+            send_attended(1, k, h + side, k)
 
 
     def sliced(v):
@@ -416,25 +424,15 @@
         pl.when(h == 0)(lambda: blank(0))
         pl.when(h == S - 1)(lambda: blank(2))
 
-    def row_in(row, k, own, outermost):
-        lacks_one = outermost | (own & (t == k))
-
-        @pl.when(lacks_one)
-        def _():
-            drain(dall.at[pl.ds(0, C - 1)], dsem.at[row, k])
-
-        @pl.when(jnp.logical_not(lacks_one))
-        def _():
-            drain(dall.at[pl.ds(0, C)], dsem.at[row, k])
-
-        activate(row, k)
-
     def block_in(k):
         if k:
-            pl.when(jnp.logical_not(attends) & (t >= k))(lambda: forward(k))
-        row_in(1, k, attends, jnp.logical_not(attends))
-        pl.when(h > 0)(lambda: row_in(0, k, h == 1, h == S - 1))
-        pl.when(h < S - 1)(lambda: row_in(2, k, h == S - 2, h == 0))
+            pl.when(t >= k)(lambda: forward(k))
+        for row, there, _ in rows:
+
+            @pl.when(there)
+            def _():
+                drain(dall.at[pl.ds(0, C - 1)], dsem.at[row, k])
+                activate(row, k)
 
     wide = half // CHUNKS
 
@@ -507,13 +505,15 @@
 
     @pl.when(attends & jnp.logical_not(at_edge))
     def _():
-        drain(dall.at[pl.ds(0, 3 * NF - 1)], dsend.at[1])
+        drain(dall.at[pl.ds(0, 3 * T + C - 2)], dsend.at[1])
+        drain(dall.at[pl.ds(0, (3 * T - 1) * (C - 1))], share_sem)
         drain(att_src.at[0, 0], asend)
 
     @pl.when(at_edge)
     def _():
-        drain(dall.at[pl.ds(0, 2 * T)], dsend.at[0])
-        drain(dall.at[pl.ds(0, 3 * NF - 2)], dsend.at[1])
+        drain(dall.at[pl.ds(0, 2)], dsend.at[2])
+        drain(dall.at[pl.ds(0, 3 * T + 2 * C - 4)], dsend.at[1])
+        drain(dall.at[pl.ds(0, (3 * T - 2) * (C - 1))], share_sem)
         drain(xall.at[pl.ds(0, C + 1)], asend)
 
     drain(gall.at[pl.ds(0, C - 1)], gsend)
@@ -597,9 +597,9 @@
             dma(()),
             dma(()),
             dma(()),
-            dma((2,)),
+            dma((3,)),
             dma((3, T)),
-            dma((2, T)),
+            dma((3, T)),
             dma(()),
             dma(()),
             dma((links, CHUNKS)),

time: 20.8 us -> 20.5 us (0.986)
  no operation moved by 1% of the time
where the time goes in v8:
time: 20.5 us; the launch traced here: 20.4 us
  Pallas kernels  19.7 us (96%)
  between operations  0.64 us (3%)
    pallas_call x1, Pallas kernels, on_device(): pl.pallas_call(functools.partial(kernel, S, T, C, W), out_shape=(kept, ke...  19.1 us
    pallas_call x1, Pallas kernels, on_device(): pl.pallas_call(hand_over, out_shape=(out, out), in_specs=[vmem] * 2, out_...  0.66 us

profile of v8, /device:TPU:0, one launch (start us, length us, event | category | flops | bytes accessed | tf_op | source)
XLA Modules:
  0.0 20.4 jit_solution(6425805451439448631)
XLA Ops:
  0.6 19.1 %shard_map.95 = (bf16[2,1,64,256]{3,2,1,0:T(8,128)(2,1)S(1)}, bf16[2,1,64,256]{3,2,1,0:T(8,128)(2,1)S(1)}) custom-call(bf16[2,1,64,256]{3,2,1,0:T(8,128)(2,1)} %x_hbm.1, f32[1,256]{1,0:T(1,128)} %bitcast.4, f32[1,256]{1,0:T(1,128)} %bitcast.5, bf16[512,512]{1,0:T(8,128)(2,1)} %wq_hbm.1, bf16[512,512]{1,0:T(8,128)(2,1)} %wk_hbm.1, bf16[512,512]{1,0:T(8,128)(2,1)} %wv_hbm.1, ...), custom_call_target="tpu_custom_call" | custom-call | tf_op jit(solution)/shard_map/pallas_call | solution.py:558
  19.7 0.7 %shard_map.96 = (bf16[2,1,64,256]{3,2,1,0:T(8,128)(2,1)}, bf16[2,1,64,256]{3,2,1,0:T(8,128)(2,1)}) custom-call(bf16[2,1,64,256]{3,2,1,0:T(8,128)(2,1)S(1)} %get-tuple-element.4.att_in, bf16[2,1,64,256]{3,2,1,0:T(8,128)(2,1)S(1)} %get-tuple-element.5.conv_in), custom_call_target="tpu_custom_call" | custom-call | tf_op jit(solution)/shard_map/pallas_call | solution.py:609

commit v9 on v8

--- a/solution.py
+++ b/solution.py
@@ -338,6 +338,12 @@
         if R == 2:
             for i in range(2):
                 send_row(i, outer, others, dsend.at[0])
+
+            def own_column():
+                for i in range(2):
+                    send_row(i, outer, [0], dsend.at[2])
+
+            pl.when(t == 0)(own_column)
             send_row(0, h - side, [*others, 0], dsend.at[1])
         else:
             for r in (h - 1, h + 1):
@@ -355,8 +361,7 @@
         if R == 2:
             if T > 1:
                 drain(dall.at[pl.ds(0, 2 * (T - 1))], dsend.at[0])
-            for i in range(2):
-                send_row(i, outer, [0], dsend.at[2])
+            pl.when(t > 0)(own_column)
 
     if S > 4:
         pl.when(attends & jnp.logical_not(at_edge))(lambda: attend(1))
@@ -377,8 +382,6 @@
 
 
     forward(0)
-    for k in range(1, T):
-        pl.when(t < k)(lambda: forward(k))
 
     @pl.when(jnp.logical_not(attends))
     def _():
@@ -404,6 +407,9 @@
     mean2, scale2 = slice_moments(jnp.sum(stat2[0:attending], axis=0), population)
     factor2 = scale2 * sliced(gain2)
     column = lax.broadcasted_iota(jnp.int32, (W, Kc), 0)
+    for k in range(1, T):
+        pl.when(t < k)(lambda: forward(k))
+
 
     def activate(row, k):
         for f in range(k * C, (k + 1) * C):

time: 20.5 us -> 20.6 us (level)
  the two profiles are of different devices: /device:TPU:0 before, /device:TPU:7 now
where the time goes in v9:
time: 20.6 us; the launch traced here: 20.4 us
  Pallas kernels  19.8 us (96%)
  between operations  0.64 us (3%)
    pallas_call x1, Pallas kernels, on_device(): pl.pallas_call(functools.partial(kernel, S, T, C, W), out_shape=(kept, ke...  19.1 us
    pallas_call x1, Pallas kernels, on_device(): pl.pallas_call(hand_over, out_shape=(out, out), in_specs=[vmem] * 2, out_...  0.66 us

profile of v9, /device:TPU:7, one launch (start us, length us, event | category | flops | bytes accessed | tf_op | source)
XLA Modules:
  0.0 20.4 jit_solution(17669065137290403017)
XLA Ops:
  0.6 19.1 %shard_map.95 = (bf16[2,1,64,256]{3,2,1,0:T(8,128)(2,1)S(1)}, bf16[2,1,64,256]{3,2,1,0:T(8,128)(2,1)S(1)}) custom-call(bf16[2,1,64,256]{3,2,1,0:T(8,128)(2,1)} %x_hbm.1, f32[1,256]{1,0:T(1,128)} %bitcast.4, f32[1,256]{1,0:T(1,128)} %bitcast.5, bf16[512,512]{1,0:T(8,128)(2,1)} %wq_hbm.1, bf16[512,512]{1,0:T(8,128)(2,1)} %wk_hbm.1, bf16[512,512]{1,0:T(8,128)(2,1)} %wv_hbm.1, ...), custom_call_target="tpu_custom_call" | custom-call | tf_op jit(solution)/shard_map/pallas_call | solution.py:564
  19.8 0.7 %shard_map.96 = (bf16[2,1,64,256]{3,2,1,0:T(8,128)(2,1)}, bf16[2,1,64,256]{3,2,1,0:T(8,128)(2,1)}) custom-call(bf16[2,1,64,256]{3,2,1,0:T(8,128)(2,1)S(1)} %get-tuple-element.4.att_in, bf16[2,1,64,256]{3,2,1,0:T(8,128)(2,1)S(1)} %get-tuple-element.5.conv_in), custom_call_target="tpu_custom_call" | custom-call | tf_op jit(solution)/shard_map/pallas_call | solution.py:615

commit v10 on v9

--- a/solution.py
+++ b/solution.py
@@ -148,12 +148,6 @@
         for i, (src, dst) in zip((0, 0, 0, 1, 2), [(wq_hbm, projections.at[0]), (wk_hbm, projections.at[1]), (wv_hbm, projections.at[2]), (wo_hbm, wo), (wc_hbm, wc)])
     ]
 
-    @pl.when(attends)
-    def _():
-        for load in loads[:4]:
-            load.start()
-
-    loads[4].start()
 
     x_load.wait()
     store_sums(stat1_src, x[...].reshape(C * W, half).astype(F32))
@@ -204,6 +198,12 @@
 
     drain(gall.at[c], xload.at[1])
     mates(lambda where: send(gall.at[c], gall.at[c], gsend, gsem, where))
+    @pl.when(attends)
+    def _():
+        for load in loads[:4]:
+            load.start()
+
+    loads[4].start()
 
     @pl.when(h < S - 2)
     def _():
@@ -330,20 +330,28 @@
         def send_stat2(where):
             send(stat2_src.at[where[2]], stat2.at[me], s2send, s2sem, where)
 
-        rows_apart(-1, lambda r, d: row_devices(r, send_stat2))
-        rows_apart(1, lambda r, d: row_devices(r, send_stat2))
+        if R == 2:
+            row_devices(outer, send_stat2)
+            for i in range(2):
+                send_row(i, outer, others, dsend.at[0])
+
+            def own_column():
+                for i in range(2):
+                    send_row(i, outer, [0], dsend.at[2])
+
+            pl.when(t == 0)(own_column)
+        def beyond_outer(r, d):
+            if R == 2:
+                pl.when(r != outer)(lambda: row_devices(r, send_stat2))
+            else:
+                row_devices(r, send_stat2)
+
+        rows_apart(-1, beyond_outer)
+        rows_apart(1, beyond_outer)
         beside(-1, send_stat2)
         beside(1, send_stat2)
         mates(send_stat2)
         if R == 2:
-            for i in range(2):
-                send_row(i, outer, others, dsend.at[0])
-
-            def own_column():
-                for i in range(2):
-                    send_row(i, outer, [0], dsend.at[2])
-
-            pl.when(t == 0)(own_column)
             send_row(0, h - side, [*others, 0], dsend.at[1])
         else:
             for r in (h - 1, h + 1):
@@ -407,9 +415,6 @@
     mean2, scale2 = slice_moments(jnp.sum(stat2[0:attending], axis=0), population)
     factor2 = scale2 * sliced(gain2)
     column = lax.broadcasted_iota(jnp.int32, (W, Kc), 0)
-    for k in range(1, T):
-        pl.when(t < k)(lambda: forward(k))
-
 
     def activate(row, k):
         for f in range(k * C, (k + 1) * C):
@@ -477,9 +482,15 @@
     def keep(chunk, value):
         own_total[chunk] = value
 
+    pl.when(c == 0)(lambda: block_in(0))
+    for k in range(1, T):
+        pl.when(t < k)(lambda: forward(k))
+
+    pl.when(c > 0)(lambda: block_in(0))
     loads[4].wait()
     for k in range(T):
-        block_in(k)
+        if k:
+            block_in(k)
         pl.when(t != k)(lambda: convolve_away(k))
 
     for k in range(T):

time: 20.6 us -> 20.4 us (level)
  the two profiles are of different devices: /device:TPU:7 before, /device:TPU:0 now
where the time goes in v10:
time: 20.4 us; the launch traced here: 20.2 us
  Pallas kernels  19.6 us (96%)
  between operations  0.64 us (3%)
    pallas_call x1, Pallas kernels, on_device(): pl.pallas_call(functools.partial(kernel, S, T, C, W), out_shape=(kept, ke...  18.9 us
    pallas_call x1, Pallas kernels, on_device(): pl.pallas_call(hand_over, out_shape=(out, out), in_specs=[vmem] * 2, out_...  0.66 us

profile of v10, /device:TPU:0, one launch (start us, length us, event | category | flops | bytes accessed | tf_op | source)
XLA Modules:
  0.0 20.2 jit_solution(15764335762790806151)
XLA Ops:
  0.6 18.9 %shard_map.95 = (bf16[2,1,64,256]{3,2,1,0:T(8,128)(2,1)S(1)}, bf16[2,1,64,256]{3,2,1,0:T(8,128)(2,1)S(1)}) custom-call(bf16[2,1,64,256]{3,2,1,0:T(8,128)(2,1)} %x_hbm.1, f32[1,256]{1,0:T(1,128)} %bitcast.4, f32[1,256]{1,0:T(1,128)} %bitcast.5, bf16[512,512]{1,0:T(8,128)(2,1)} %wq_hbm.1, bf16[512,512]{1,0:T(8,128)(2,1)} %wk_hbm.1, bf16[512,512]{1,0:T(8,128)(2,1)} %wv_hbm.1, ...), custom_call_target="tpu_custom_call" | custom-call | tf_op jit(solution)/shard_map/pallas_call | solution.py:575
  19.6 0.7 %shard_map.96 = (bf16[2,1,64,256]{3,2,1,0:T(8,128)(2,1)}, bf16[2,1,64,256]{3,2,1,0:T(8,128)(2,1)}) custom-call(bf16[2,1,64,256]{3,2,1,0:T(8,128)(2,1)S(1)} %get-tuple-element.4.att_in, bf16[2,1,64,256]{3,2,1,0:T(8,128)(2,1)S(1)} %get-tuple-element.5.conv_in), custom_call_target="tpu_custom_call" | custom-call | tf_op jit(solution)/shard_map/pallas_call | solution.py:626

commit v11 on v10

--- a/solution.py
+++ b/solution.py
@@ -61,11 +61,11 @@
     S, T, C, W,
     x_hbm, g1, g2, wq_hbm, wk_hbm, wv_hbm, wo_hbm, wc_hbm,
     att_out, conv_out,
-    x, projections, wo, wc,
+    x, projections, wc,
     stat1_src, row_sum, stat1, stat2_src, stat2, gall,
     xall, tokens, keyed, valued, att_src, att_in, dsrc, dall, act, own_total, part_src, part,
     xload, wsem, insem, gsend, gsem, raw_sem, s1send, s1sem, xsend, xsem, s2send, s2sem,
-    asend, asem, dsend, dsem, direct_sem, share_sem, psend, psem,
+    asend, asem, dsend, dsem, direct_sem, psend, psem,
 ):
     g = lax.axis_index("groups")
     h = lax.axis_index("space")
@@ -145,7 +145,7 @@
 
     loads = [
         pltpu.make_async_copy(src, dst, wsem.at[i])
-        for i, (src, dst) in zip((0, 0, 0, 1, 2), [(wq_hbm, projections.at[0]), (wk_hbm, projections.at[1]), (wv_hbm, projections.at[2]), (wo_hbm, wo), (wc_hbm, wc)])
+        for i, (src, dst) in zip((0, 0, 0, 0, 1), [(wq_hbm, projections.at[0]), (wk_hbm, projections.at[1]), (wv_hbm, projections.at[2]), (wo_hbm, projections.at[3]), (wc_hbm, wc)])
     ]
 
 
@@ -170,7 +170,7 @@
 
     def send_x(r, dc):
         frame = lax.rem(c + dc, C)
-        send(x.at[frame, 0], xall.at[h * C + c], xsend, xsem.at[h], (g, r, t, frame))
+        send(x.at[frame, 0], xall.at[h * C + c], xsend, xsem, (g, r, t, frame))
 
     def column_x(r):
         for dc in range(C):
@@ -258,22 +258,14 @@
         def rest(i):
             return i + skipped if R == 2 else i + jnp.where(i >= h, 1, 0)
 
-        def slots_in(r):
-            drain(xall.at[pl.ds(r * C, C)], xsem.at[r])
-
         for r in range(1, S - 1):
 
             @pl.when(h == r)
             def _():
                 drain(stat1.at[pl.ds(0, r * C + T * (C - 1) + (S - 1 - r) * T * C)], s1sem)
 
-        drain(xall.at[pl.ds(0, C - 1)], xsem.at[h])
-        if R == 2:
-            slots_in(outer)
-        for i in range(S - R):
-            slots_in(rest(i))
+        drain(xall.at[pl.ds(0, S * C - 1)], xsem)
         drain(projections, wsem.at[0])
-        drain(wo, wsem.at[1])
         totals = jnp.sum(stat1[...].reshape(S * T, C, *stat1.shape[1:]), axis=0)
         mean1, scale1 = moments([totals[k] for k in range(C)], population)
         factor1 = scale1 * jnp.concatenate([gall[k, 0] for k in range(C)], axis=1)
@@ -305,7 +297,7 @@
         mass = jnp.sum(weights, axis=1, keepdims=True)
         mixed = jnp.dot(weights.astype(BF16), valued[...], preferred_element_type=F32)
         mixed = (mixed * (1.0 / mass)).astype(BF16)
-        attended = jnp.dot(mixed, wo[...], preferred_element_type=F32).astype(BF16)
+        attended = jnp.dot(mixed, projections[3], preferred_element_type=F32).astype(BF16)
 
         source = jnp.concatenate(
             [jnp.concatenate([xall[r * C + k] for k in range(C)], axis=1) for r in mine], axis=0
@@ -337,7 +329,7 @@
 
             def own_column():
                 for i in range(2):
-                    send_row(i, outer, [0], dsend.at[2])
+                    send_row(i, outer, [0], dsend.at[1])
 
             pl.when(t == 0)(own_column)
         def beyond_outer(r, d):
@@ -386,7 +378,7 @@
             def _():
                 slot = row * NF + k * C + c
                 drain(dall.at[slot], direct_sem.at[row, k])
-                mates(lambda where: send(dall.at[slot], dall.at[slot], share_sem, dsem.at[row, k], where))
+                mates(lambda where: send(dall.at[slot], dall.at[slot], dsend.at[1], dsem.at[row, k], where))
 
 
     forward(0)
@@ -509,7 +501,7 @@
         for k in range(C):
             att_out[k, 0] = att_in[k]
         drain(xall.at[pl.ds(0, (S - 2) * C)], xsend)
-        drain(dall.at[pl.ds(0, 2 * T * (C - 1))], share_sem)
+        drain(dall.at[pl.ds(0, 2 * T * (C - 1))], dsend.at[1])
 
     for r in range(S):
 
@@ -522,15 +514,12 @@
 
     @pl.when(attends & jnp.logical_not(at_edge))
     def _():
-        drain(dall.at[pl.ds(0, 3 * T + C - 2)], dsend.at[1])
-        drain(dall.at[pl.ds(0, (3 * T - 1) * (C - 1))], share_sem)
+        drain(dall.at[pl.ds(0, 3 * T + C - 2 + (3 * T - 1) * (C - 1))], dsend.at[1])
         drain(att_src.at[0, 0], asend)
 
     @pl.when(at_edge)
     def _():
-        drain(dall.at[pl.ds(0, 2)], dsend.at[2])
-        drain(dall.at[pl.ds(0, 3 * T + 2 * C - 4)], dsend.at[1])
-        drain(dall.at[pl.ds(0, (3 * T - 2) * (C - 1))], share_sem)
+        drain(dall.at[pl.ds(0, 3 * T + 2 * C - 2 + (3 * T - 2) * (C - 1))], dsend.at[1])
         drain(xall.at[pl.ds(0, C + 1)], asend)
 
     drain(gall.at[pl.ds(0, C - 1)], gsend)
@@ -579,8 +568,7 @@
         out_specs=(vmem, vmem),
         scratch_shapes=[
             pltpu.VMEM(x.shape, BF16),
-            pltpu.VMEM((3, D, D), BF16),
-            pltpu.VMEM((D, D), BF16),
+            pltpu.VMEM((4, D, D), BF16),
             pltpu.VMEM(wc.shape, BF16),
             pltpu.VMEM((half // 64, LANES), F32),
             pltpu.VMEM((half // 64, LANES), F32),
@@ -601,7 +589,7 @@
             pltpu.VMEM((links, CHUNKS, C * W, wide), BF16),
             pltpu.VMEM((links, CHUNKS, C * W, wide), BF16),
             dma((2,)),
-            dma((3,)),
+            dma((2,)),
             pltpu.SemaphoreType.REGULAR((S - 1,)),
             dma(()),
             dma(()),
@@ -609,15 +597,14 @@
             dma(()),
             dma(()),
             dma(()),
-            dma((S,)),
-            dma(()),
-            dma(()),
-            dma(()),
-            dma(()),
-            dma((3,)),
+            dma(()),
+            dma(()),
+            dma(()),
+            dma(()),
+            dma(()),
+            dma((2,)),
             dma((3, T)),
             dma((3, T)),
-            dma(()),
             dma(()),
             dma((links, CHUNKS)),
         ],

time: 20.4 us -> 20.4 us (level)
  no operation moved by 1% of the time
where the time goes in v11:
time: 20.4 us; the launch traced here: 20.1 us
  Pallas kernels  19.5 us (96%)
  between operations  0.64 us (3%)
    pallas_call x1, Pallas kernels, on_device(): pl.pallas_call(functools.partial(kernel, S, T, C, W), out_shape=(kept, ke...  18.8 us
    pallas_call x1, Pallas kernels, on_device(): pl.pallas_call(hand_over, out_shape=(out, out), in_specs=[vmem] * 2, out_...  0.66 us

profile of v11, /device:TPU:0, one launch (start us, length us, event | category | flops | bytes accessed | tf_op | source)
XLA Modules:
  0.0 20.1 jit_solution(4808253270428172799)
XLA Ops:
  0.6 18.8 %shard_map.95 = (bf16[2,1,64,256]{3,2,1,0:T(8,128)(2,1)S(1)}, bf16[2,1,64,256]{3,2,1,0:T(8,128)(2,1)S(1)}) custom-call(bf16[2,1,64,256]{3,2,1,0:T(8,128)(2,1)} %x_hbm.1, f32[1,256]{1,0:T(1,128)} %bitcast.4, f32[1,256]{1,0:T(1,128)} %bitcast.5, bf16[512,512]{1,0:T(8,128)(2,1)} %wq_hbm.1, bf16[512,512]{1,0:T(8,128)(2,1)} %wk_hbm.1, bf16[512,512]{1,0:T(8,128)(2,1)} %wv_hbm.1, ...), custom_call_target="tpu_custom_call" | custom-call | tf_op jit(solution)/shard_map/pallas_call | solution.py:564
  19.5 0.7 %shard_map.96 = (bf16[2,1,64,256]{3,2,1,0:T(8,128)(2,1)}, bf16[2,1,64,256]{3,2,1,0:T(8,128)(2,1)}) custom-call(bf16[2,1,64,256]{3,2,1,0:T(8,128)(2,1)S(1)} %get-tuple-element.4.att_in, bf16[2,1,64,256]{3,2,1,0:T(8,128)(2,1)S(1)} %get-tuple-element.5.conv_in), custom_call_target="tpu_custom_call" | custom-call | tf_op jit(solution)/shard_map/pallas_call | solution.py:613

commit v12 on v11

--- a/solution.py
+++ b/solution.py
@@ -194,7 +194,7 @@
             send_x(h, dc)
 
     for r in range(1, S - 1):
-        pl.when(r < h)(lambda: column_x(r))
+        pl.when((r < h) & ((h < S - 1) | (r < S - 2)))(lambda: column_x(r))
 
     drain(gall.at[c], xload.at[1])
     mates(lambda where: send(gall.at[c], gall.at[c], gsend, gsem, where))
@@ -217,6 +217,7 @@
             pl.when(r < h)(lambda: row_where(r, 1, send_stat))
         pl.when(h < S - 1)(lambda: same_row(1))
 
+    pl.when(h == S - 1)(lambda: column_x(S - 2))
     @pl.when(h < S - 1)
     def _():
         if T > 1:
@@ -382,6 +383,9 @@
 
 
     forward(0)
+    for k in range(1, T):
+        pl.when((t < k) & (c > 0))(lambda: forward(k))
+
 
     @pl.when(jnp.logical_not(attends))
     def _():
@@ -476,7 +480,7 @@
 
     pl.when(c == 0)(lambda: block_in(0))
     for k in range(1, T):
-        pl.when(t < k)(lambda: forward(k))
+        pl.when((t < k) & (c == 0))(lambda: forward(k))
 
     pl.when(c > 0)(lambda: block_in(0))
     loads[4].wait()

time: 20.4 us -> 20.3 us (level)
  no operation moved by 1% of the time
where the time goes in v12:
time: 20.3 us; the launch traced here: 20.1 us
  Pallas kernels  19.5 us (96%)
  between operations  0.64 us (3%)
    pallas_call x1, Pallas kernels, on_device(): pl.pallas_call(functools.partial(kernel, S, T, C, W), out_shape=(kept, ke...  18.8 us
    pallas_call x1, Pallas kernels, on_device(): pl.pallas_call(hand_over, out_shape=(out, out), in_specs=[vmem] * 2, out_...  0.66 us

profile of v12, /device:TPU:0, one launch (start us, length us, event | category | flops | bytes accessed | tf_op | source)
XLA Modules:
  0.0 20.1 jit_solution(17016568284087140027)
XLA Ops:
  0.6 18.8 %shard_map.95 = (bf16[2,1,64,256]{3,2,1,0:T(8,128)(2,1)S(1)}, bf16[2,1,64,256]{3,2,1,0:T(8,128)(2,1)S(1)}) custom-call(bf16[2,1,64,256]{3,2,1,0:T(8,128)(2,1)} %x_hbm.1, f32[1,256]{1,0:T(1,128)} %bitcast.4, f32[1,256]{1,0:T(1,128)} %bitcast.5, bf16[512,512]{1,0:T(8,128)(2,1)} %wq_hbm.1, bf16[512,512]{1,0:T(8,128)(2,1)} %wk_hbm.1, bf16[512,512]{1,0:T(8,128)(2,1)} %wv_hbm.1, ...), custom_call_target="tpu_custom_call" | custom-call | tf_op jit(solution)/shard_map/pallas_call | solution.py:568
  19.5 0.7 %shard_map.96 = (bf16[2,1,64,256]{3,2,1,0:T(8,128)(2,1)}, bf16[2,1,64,256]{3,2,1,0:T(8,128)(2,1)}) custom-call(bf16[2,1,64,256]{3,2,1,0:T(8,128)(2,1)S(1)} %get-tuple-element.4.att_in, bf16[2,1,64,256]{3,2,1,0:T(8,128)(2,1)S(1)} %get-tuple-element.5.conv_in), custom_call_target="tpu_custom_call" | custom-call | tf_op jit(solution)/shard_map/pallas_call | solution.py:617

commit v13 on v12

--- a/solution.py
+++ b/solution.py
@@ -11,7 +11,7 @@
 NGROUP = 32
 EPSILON = 1e-06
 LANES = 128
-CHUNKS = 2
+CHUNKS = 1
 GROUP = D // NGROUP
 MESH = pl.DeviceIdType.MESH
 F32 = jnp.float32

time: 20.3 us -> 20.3 us (level)
  no operation moved by 1% of the time
where the time goes in v13:
time: 20.3 us; the launch traced here: 20.2 us
  Pallas kernels  19.5 us (96%)
  between operations  0.64 us (3%)
    pallas_call x1, Pallas kernels, on_device(): pl.pallas_call(functools.partial(kernel, S, T, C, W), out_shape=(kept, ke...  18.9 us
    pallas_call x1, Pallas kernels, on_device(): pl.pallas_call(hand_over, out_shape=(out, out), in_specs=[vmem] * 2, out_...  0.66 us

profile of v13, /device:TPU:0, one launch (start us, length us, event | category | flops | bytes accessed | tf_op | source)
XLA Modules:
  0.0 20.2 jit_solution(5180694827034445667)
XLA Ops:
  0.6 18.9 %shard_map.95 = (bf16[2,1,64,256]{3,2,1,0:T(8,128)(2,1)S(1)}, bf16[2,1,64,256]{3,2,1,0:T(8,128)(2,1)S(1)}) custom-call(bf16[2,1,64,256]{3,2,1,0:T(8,128)(2,1)} %x_hbm.1, f32[1,256]{1,0:T(1,128)} %bitcast.4, f32[1,256]{1,0:T(1,128)} %bitcast.5, bf16[512,512]{1,0:T(8,128)(2,1)} %wq_hbm.1, bf16[512,512]{1,0:T(8,128)(2,1)} %wk_hbm.1, bf16[512,512]{1,0:T(8,128)(2,1)} %wv_hbm.1, ...), custom_call_target="tpu_custom_call" | custom-call | tf_op jit(solution)/shard_map/pallas_call | solution.py:568
  19.5 0.7 %shard_map.96 = (bf16[2,1,64,256]{3,2,1,0:T(8,128)(2,1)}, bf16[2,1,64,256]{3,2,1,0:T(8,128)(2,1)}) custom-call(bf16[2,1,64,256]{3,2,1,0:T(8,128)(2,1)S(1)} %get-tuple-element.4.att_in, bf16[2,1,64,256]{3,2,1,0:T(8,128)(2,1)S(1)} %get-tuple-element.5.conv_in), custom_call_target="tpu_custom_call" | custom-call | tf_op jit(solution)/shard_map/pallas_call | solution.py:617
